TPU v7x, 32 devices: a whole 2x2x4 slice. The times are simulated.
32 devices in a mesh: dp: 8 (over y, x, core), mp: 4 (over z).
Axes of the slice: x: 2, y: 2, z: 4, core: 2. Of those that a mesh axis runs over, the one named last changes fastest.
Arguments:
- inputs: bfloat16 [8192, 2048], P('dp'), may hold values from -8 to 8
- segment_ids: int32 [8, 1024], P('dp'), may hold values from 0 to 4, as said below
- pad_count: int32 [8], P('dp'), may hold values from 0 to 128, as said below
- layer_norm_gain: float32 [2048], replicated, may hold values from 0.5 to 1.5
- layer_norm_bias: float32 [2048], replicated, may hold values from -1.75 to 1.75
- qkv_weight: bfloat16 [2048, 3, 2048], P(None, None, 'mp'), may hold values from -0.125 to 0.125
- qkv_bias: float32 [3, 2048], P(None, 'mp'), may hold values from -1.75 to 1.75
- out_weight: bfloat16 [2048, 2048], P('mp'), may hold values from -1 to 1
- gateup_weight: bfloat16 [2048, 2, 5632], P(None, None, 'mp'), may hold values from -0.125 to 0.125
- down_weight: bfloat16 [5632, 2048], P('mp'), may hold values from -0.078125 to 0.078125
- y_grad: bfloat16 [8192, 2048], P('dp'), may hold values from -8 to 8
Outputs:
- output: bfloat16 [8192, 2048], P('dp')
- x_grad: bfloat16 [8192, 2048], P('dp')
- ln_gain_grad: float32 [2048], replicated
- ln_bias_grad: float32 [2048], replicated
- qkv_weight_grad: float32 [2048, 3, 2048], P('dp', None, 'mp')
- qkv_bias_grad: float32 [3, 2048], P(None, 'mp')
- out_weight_grad: float32 [2048, 2048], P('mp', 'dp')
- gateup_weight_grad: float32 [2048, 2, 5632], P('dp', None, 'mp')
- down_weight_grad: float32 [5632, 2048], P('mp', 'dp')
Inputs may be any that keep to these rules, and one draw needn't show every extreme that they name: `segment_ids`: within a row the ids never fall and run from 0 to 4 - 1 over the row's documents, each of 1 or more tokens and one of exactly 512; the row's last pad_count slots carry id 4. `pad_count`: some row has 128 padded slots and some row has none.
All inputs are finite; a program needn't handle non-finite values.
Results may differ from a plain program's by a relative error of at most 0.012.
The roundings to bfloat16 on the way count: a program that leaves them out, or rounds other values in their place, can miss the bound.
Values may be sent and summed in bfloat16 or wider, within the bound.
No kernel may reach another device: no remote copies, remote signals or barrier semaphores. Data moves between devices by JAX's collectives and lax.ppermute only.
A program may use at most 256 MiB of HBM per device.

v0:
```python
import jax
import jax.numpy as jnp
from jax import lax
from jax.sharding import PartitionSpec as P

HEAD_DIM = 64
ROT = 16
DOCS = 4


EPS = 1e-05


def tables(seg, padding, count):
    steps = jnp.arange(count, dtype=jnp.int32)
    onehot = (seg[:, None] == jnp.arange(DOCS + 1, dtype=jnp.int32)[None, :]).astype(jnp.int32)
    counts = jnp.sum(onehot, axis=0)
    before = jnp.cumsum(counts) - counts
    start = jnp.sum(onehot * before[None, :], axis=1)
    half = ROT // 2
    freq = jnp.power(10000.0, -2.0 * jnp.arange(half, dtype=jnp.float32) / ROT)
    angle = (steps - start).astype(jnp.float32)[:, None] * freq[None, :]
    return (jnp.cos(angle)[:, None, :], jnp.sin(angle)[:, None, :], steps < count - padding)


def rotate(value, cosine, sine):
    half = ROT // 2
    first = value[..., :half]
    second = value[..., half:ROT]
    return jnp.concatenate(
        [first * cosine - second * sine, second * cosine + first * sine, value[..., ROT:]], axis=-1
    )


def unrotate(value, cosine, sine):
    half = ROT // 2
    first = value[..., :half]
    second = value[..., half:ROT]
    return jnp.concatenate(
        [first * cosine + second * sine, second * cosine - first * sine, value[..., ROT:]], axis=-1
    )


def allowed_mask(start, block_rows, seg, valid):
    count = seg.shape[0]
    rows = start + jnp.arange(block_rows, dtype=jnp.int32)
    cols = jnp.arange(count, dtype=jnp.int32)
    seg_rows = lax.dynamic_slice_in_dim(seg, start, block_rows, 0)
    allowed = (
        (seg_rows[:, None] == seg[None, :]) & (cols[None, :] <= rows[:, None]) & valid[None, :]
    )
    return allowed | (cols[None, :] == rows[:, None])


def scores(start, block_rows, query, key, seg, valid):
    part = lax.dynamic_slice_in_dim(query, start, block_rows, 0)
    score = jnp.einsum(
        "qhd,khd->hqk", part, key, preferred_element_type=jnp.float32
    ) * HEAD_DIM ** (-0.5)
    allowed = allowed_mask(start, block_rows, seg, valid)
    return (part, jnp.where(allowed[None], score, -1e30), allowed)


def shards(
    inputs,
    segment_ids,
    pad_count,
    layer_norm_gain,
    layer_norm_bias,
    qkv_weight,
    qkv_bias,
    out_weight,
    gateup_weight,
    down_weight,
    y_grad,
):
    count, width = inputs.shape
    local = qkv_weight.shape[2]
    hidden_here = gateup_weight.shape[2]
    heads_here = local // HEAD_DIM
    seg = segment_ids[0]
    cosine, sine, valid = tables(seg, pad_count[0], count)
    valid_f = valid.astype(jnp.float32)
    xf = inputs.astype(jnp.float32)
    row_average = jnp.mean(xf, axis=-1, keepdims=True)
    mean_removed = xf - row_average
    var = jnp.mean(mean_removed * mean_removed, axis=-1, keepdims=True)
    inverse_deviation = lax.rsqrt(var + EPS)
    standardized_input = mean_removed * inverse_deviation
    norm_output = (standardized_input * layer_norm_gain + layer_norm_bias).astype(jnp.bfloat16)
    qkv = jnp.dot(
        norm_output, qkv_weight.reshape(width, 3 * local), preferred_element_type=jnp.float32
    )
    qkv = qkv.reshape(count, 3, local) + qkv_bias
    query = rotate(qkv[:, 0].reshape(count, heads_here, HEAD_DIM), cosine, sine).astype(
        jnp.bfloat16
    )
    key = rotate(qkv[:, 1].reshape(count, heads_here, HEAD_DIM), cosine, sine).astype(jnp.bfloat16)
    value = qkv[:, 2].reshape(count, heads_here, HEAD_DIM).astype(jnp.bfloat16)
    block_rows = min(512, count)
    starts = jnp.arange(count // block_rows, dtype=jnp.int32) * block_rows

    def forward_block(start):
        part, score, allowed = scores(start, block_rows, query, key, seg, valid)
        top = jnp.max(score, axis=-1, keepdims=True)
        expo = jnp.exp(score - top)
        total = jnp.sum(expo, axis=-1, keepdims=True)
        prob = (expo / total).astype(jnp.bfloat16)
        return (
            jnp.einsum("hqk,khd->qhd", prob, value, preferred_element_type=jnp.float32),
            (top + jnp.log(total))[..., 0],
        )

    attn_blocks, log_sums = lax.map(forward_block, starts)
    attn = (attn_blocks.reshape(count, local) * valid_f[:, None]).astype(jnp.bfloat16)
    gateup = jnp.dot(
        norm_output,
        gateup_weight.reshape(width, 2 * hidden_here),
        preferred_element_type=jnp.float32,
    )
    gateup = gateup.reshape(count, 2, hidden_here)
    gate = gateup[:, 0]
    upper = gateup[:, 1]
    sigma = jax.nn.sigmoid(gate)
    active = gate * sigma
    hidden = (active * upper).astype(jnp.bfloat16)
    partial_value = jnp.dot(attn, out_weight, preferred_element_type=jnp.float32) + jnp.dot(
        hidden, down_weight, preferred_element_type=jnp.float32
    )
    summed = lax.psum(partial_value, "mp")
    result = (xf + summed).astype(jnp.bfloat16)
    grad_out = jnp.einsum("ti,to->io", attn, y_grad, preferred_element_type=jnp.float32)
    grad_down = jnp.einsum("tf,to->fo", hidden, y_grad, preferred_element_type=jnp.float32)
    d_attn = jnp.einsum("to,io->ti", y_grad, out_weight, preferred_element_type=jnp.float32)
    d_attn = (d_attn.astype(jnp.bfloat16) * valid.astype(jnp.bfloat16)[:, None]).reshape(
        count, heads_here, HEAD_DIM
    )
    d_hidden = jnp.einsum("to,fo->tf", y_grad, down_weight, preferred_element_type=jnp.float32)
    d_gate = (d_hidden * upper * sigma * (1.0 + gate * (1.0 - sigma))).astype(jnp.bfloat16)
    d_upper = (d_hidden * active).astype(jnp.bfloat16)
    d_gateup = jnp.stack([d_gate, d_upper], axis=1)
    grad_gateup = jnp.einsum(
        "td,tjf->djf", norm_output, d_gateup, preferred_element_type=jnp.float32
    )

    def backward_block(carry, item):
        key_acc, value_acc = carry
        start, log_sum = item
        part, score, allowed = scores(start, block_rows, query, key, seg, valid)
        prob = jnp.where(allowed[None], jnp.exp(score - log_sum[..., None]), 0.0)
        prob_low = prob.astype(jnp.bfloat16)
        d_rows = lax.dynamic_slice_in_dim(d_attn, start, block_rows, 0)
        d_prob = jnp.einsum("qhd,khd->hqk", d_rows, value, preferred_element_type=jnp.float32)
        d_score = prob * (d_prob - jnp.sum(prob * d_prob, axis=-1, keepdims=True))
        d_score = d_score.astype(jnp.bfloat16)
        d_query = jnp.einsum(
            "hqk,khd->qhd", d_score, key, preferred_element_type=jnp.float32
        ) * HEAD_DIM ** (-0.5)
        key_acc = key_acc + jnp.einsum(
            "hqk,qhd->khd", d_score, part, preferred_element_type=jnp.float32
        ) * HEAD_DIM ** (-0.5)
        value_acc = value_acc + jnp.einsum(
            "hqk,qhd->khd", prob_low, d_rows, preferred_element_type=jnp.float32
        )
        return ((key_acc, value_acc), d_query)

    empty = jnp.zeros((count, heads_here, HEAD_DIM), jnp.float32)
    (d_key, d_value), d_queries = lax.scan(backward_block, (empty, empty), (starts, log_sums))
    d_query = unrotate(d_queries.reshape(count, heads_here, HEAD_DIM), cosine, sine)
    d_key = unrotate(d_key, cosine, sine)
    d_qkv = (
        jnp.stack([d_query, d_key, d_value], axis=1).reshape(count, 3, local).astype(jnp.bfloat16)
    )
    grad_qkv = jnp.einsum("td,tjc->djc", norm_output, d_qkv, preferred_element_type=jnp.float32)
    grad_bias = jnp.sum(d_qkv.astype(jnp.float32), axis=0)
    weight_sums = (
        lax.psum_scatter(grad_qkv, "dp", scatter_dimension=0, tiled=True),
        lax.psum_scatter(grad_out, "dp", scatter_dimension=1, tiled=True),
        lax.psum_scatter(grad_gateup, "dp", scatter_dimension=0, tiled=True),
        lax.psum_scatter(grad_down, "dp", scatter_dimension=1, tiled=True),
    )
    d_partial = jnp.einsum(
        "tjc,djc->td", d_qkv, qkv_weight, preferred_element_type=jnp.float32
    ) + jnp.einsum("tjf,djf->td", d_gateup, gateup_weight, preferred_element_type=jnp.float32)
    normalized_gradient = lax.psum(d_partial, "mp")
    gain_product = jnp.sum(normalized_gradient * standardized_input, axis=0)
    shift_part = jnp.sum(normalized_gradient, axis=0)
    gain_scaled = normalized_gradient * layer_norm_gain
    inner = (
        gain_scaled
        - jnp.mean(gain_scaled, axis=-1, keepdims=True)
        - standardized_input * jnp.mean(gain_scaled * standardized_input, axis=-1, keepdims=True)
    )
    input_grad = (y_grad.astype(jnp.float32) + inverse_deviation * inner).astype(jnp.bfloat16)
    bias_sum, gain_sum, shift_sum = lax.psum((grad_bias, gain_product, shift_part), "dp")
    return (
        result,
        input_grad,
        gain_sum,
        shift_sum,
        weight_sums[0],
        bias_sum,
        weight_sums[1],
        weight_sums[2],
        weight_sums[3],
    )


def solution(mesh):
    placed = (
        P("dp", None),
        P("dp", None),
        P("dp"),
        P(),
        P(),
        P(None, None, "mp"),
        P(None, "mp"),
        P("mp", None),
        P(None, None, "mp"),
        P("mp", None),
        P("dp", None),
    )
    return jax.shard_map(
        shards,
        mesh=mesh,
        in_specs=placed,
        out_specs=(
            P("dp", None),
            P("dp", None),
            P(),
            P(),
            P("dp", None, "mp"),
            P(None, "mp"),
            P("mp", "dp"),
            P("dp", None, "mp"),
            P("mp", "dp"),
        ),
        check_vma=False,
    )
```

profile of v0, /device:TPU:0, one launch (start us, length us, event | category | flops | bytes accessed | tf_op | source)
XLA Modules:
  0.0 1045.2 jit_solution(3423792791581384292)
XLA Ops:
  12.9 8.9 copy.39
  21.8 10.5 %broadcast_add_fusion = f32[1024,3,512]{0,2,1:T(8,128)S(1)} fusion(f32[3,512]{1,0:T(4,128)S(1)} %copy-done.24, bf16[2048,3,512]{0,2,1:T(8,128)(2,1)} %copy.39, bf16[1024,2048]{1,0:T(8,128)(2,1)} %param.15, f32[2048]{0:T(1024)S(1)} %copy-done.25, f32[2048]{0:T(1024)S(1)} %copy-done.21, f32[1024]{0:T(1024)S(1)} %add_rsqrt_fusion, ...), kind=kOutput, calls=%fused_computation.86 | convolution fusion | flops 6456606720 | bytes 16807936 | tf_op jit(solution)/shard_map/dot_general | solution.py:91
  45.3 78.9 %while.28 = (s32[]{:T(128)}, f32[2,512,8,64]{1,0,3,2:T(2,128)}, f32[2,8,512]{2,1,0:T(8,128)S(1)}, s32[2]{0:T(128)S(1)}, s32[1024]{0:T(1024)S(1)}, /*index=5*/s32...) while((s32[]{:T(128)}, f32[2,512,8,64]{1,0,3,2:T(2,128)}, ...), condition=%wide.region_8.9_spmd.clone, body=%wide.region_5.8_spmd.clone.sunk | while | flops 1127216640 | bytes 64635104 | solution.py:114
  65.2 19.6 %dynamic_update_slice.19 = f32[2,512,8,64]{1,0,3,2:T(2,128)} dynamic-update-slice(f32[2,512,8,64]{1,0,3,2:T(2,128)} %get-tuple-element.475, f32[1,512,8,64]{1,0,3,2:T(1,128)} %copy.73, s32[]{:T(128)} %get-tuple-element.474, s32[]{:T(128)} %constant.40.clone.1..sunk, s32[]{:T(128)} %constant.40.clone.1..sunk, s32[]{:T(128)} %constant.40.clone.1..sunk) | dynamic-update-slice | bytes 2097156 | tf_op jit(solution)/shard_map/while/body/jit(dynamic_update_index_in_dim)/dynamic_update_slice | solution.py:114
  104.5 19.6 %dynamic_update_slice.19 = f32[2,512,8,64]{1,0,3,2:T(2,128)} dynamic-update-slice(f32[2,512,8,64]{1,0,3,2:T(2,128)} %get-tuple-element.475, f32[1,512,8,64]{1,0,3,2:T(1,128)} %copy.73, s32[]{:T(128)} %get-tuple-element.474, s32[]{:T(128)} %constant.40.clone.1..sunk, s32[]{:T(128)} %constant.40.clone.1..sunk, s32[]{:T(128)} %constant.40.clone.1..sunk) | dynamic-update-slice | bytes 2097156 | tf_op jit(solution)/shard_map/while/body/jit(dynamic_update_index_in_dim)/dynamic_update_slice | solution.py:114
  131.7 159.2 %while.29 = (s32[]{:T(128)}, f32[1024,8,64]{0,2,1:T(8,128)}, f32[1024,8,64]{0,2,1:T(8,128)}, f32[2,512,8,64]{1,0,3,2:T(2,128)}, s32[2]{0:T(128)S(1)}, /*index=5*...) while((s32[]{:T(128)}, f32[1024,8,64]{0,2,1:T(8,128)}, ...), condition=%wide.region_12.13_spmd.clone, body=%wide.region_10.12_spmd.clone.sunk | while | flops 2732324352 | bytes 187793712 | solution.py:168
  136.1 9.7 fusion.130
  145.8 13.8 %multiply_reduce_fusion.3 = (f32[8,512]{1,0:T(8,128)S(1)}, f32[8,512,1024]{2,1,0:T(8,128)}) fusion(f32[8,512,1024]{2,1,0:T(8,128)} %fusion.130, f32[8,512]{1,0:T(8,128)S(1)} %dynamic-slice_bitcast_fusion.2, bf16[1024,8,64]{0,2,1:T(8,128)(2,1)S(1)} %get-tuple-element.540, bf16[1024,8,64]{0,2,1:T(8,128)(2,1)S(1)} %copy-done.4, s32[]{:T(128)S(6)} %select_n.47, ...), kind=kOutput, calls=%fused_computation.23.clone.1 | convolution fusion | flops 562032640 | bytes 35684356 | tf_op jit(solution)/shard_map/while/body/eval_jaxpr/qhd,khd->hqk/dot_general | solution.py:57
  159.5 11.3 %multiply_convert_fusion.8 = bf16[8,512,1024]{2,1,0:T(8,128)(2,1)S(1)} fusion(f32[8,512,1024]{2,1,0:T(8,128)} %get-tuple-element.459, f32[8,512,1024]{2,1,0:T(8,128)} %fusion.130, f32[8,512]{1,0:T(8,128)S(1)} %get-tuple-element.460), kind=kLoop, calls=%fused_computation.22.clone.1 | loop fusion | flops 12582912 | bytes 41959424 | tf_op jit(solution)/shard_map/while/body/eval_jaxpr/convert_element_type | solution.py:155
  175.7 19.6 %dynamic_update_slice.20 = f32[2,512,8,64]{1,0,3,2:T(2,128)} dynamic-update-slice(f32[2,512,8,64]{1,0,3,2:T(2,128)} %get-tuple-element.519, f32[1,512,8,64]{1,0,3,2:T(1,128)} %copy.74, s32[]{:T(128)} %get-tuple-element.516, s32[]{:T(128)} %constant.40.clone.1..sunk.1, s32[]{:T(128)} %constant.40.clone.1..sunk.1, s32[]{:T(128)} %constant.40.clone.1..sunk.1) | dynamic-update-slice | bytes 2097156 | tf_op jit(solution)/shard_map/while/body/jit(dynamic_update_index_in_dim)/dynamic_update_slice | solution.py:114
  202.0 8.7 bitcast_add_fusion.6
  214.8 9.7 fusion.130
  224.5 13.7 %multiply_reduce_fusion.3 = (f32[8,512]{1,0:T(8,128)S(1)}, f32[8,512,1024]{2,1,0:T(8,128)}) fusion(f32[8,512,1024]{2,1,0:T(8,128)} %fusion.130, f32[8,512]{1,0:T(8,128)S(1)} %dynamic-slice_bitcast_fusion.2, bf16[1024,8,64]{0,2,1:T(8,128)(2,1)S(1)} %get-tuple-element.540, bf16[1024,8,64]{0,2,1:T(8,128)(2,1)S(1)} %copy-done.4, s32[]{:T(128)S(6)} %select_n.47, ...), kind=kOutput, calls=%fused_computation.23.clone.1 | convolution fusion | flops 562032640 | bytes 35684356 | tf_op jit(solution)/shard_map/while/body/eval_jaxpr/qhd,khd->hqk/dot_general | solution.py:57
  238.2 11.3 %multiply_convert_fusion.8 = bf16[8,512,1024]{2,1,0:T(8,128)(2,1)S(1)} fusion(f32[8,512,1024]{2,1,0:T(8,128)} %get-tuple-element.459, f32[8,512,1024]{2,1,0:T(8,128)} %fusion.130, f32[8,512]{1,0:T(8,128)S(1)} %get-tuple-element.460), kind=kLoop, calls=%fused_computation.22.clone.1 | loop fusion | flops 12582912 | bytes 41959424 | tf_op jit(solution)/shard_map/while/body/eval_jaxpr/convert_element_type | solution.py:155
  254.4 19.6 %dynamic_update_slice.20 = f32[2,512,8,64]{1,0,3,2:T(2,128)} dynamic-update-slice(f32[2,512,8,64]{1,0,3,2:T(2,128)} %get-tuple-element.519, f32[1,512,8,64]{1,0,3,2:T(1,128)} %copy.74, s32[]{:T(128)} %get-tuple-element.516, s32[]{:T(128)} %constant.40.clone.1..sunk.1, s32[]{:T(128)} %constant.40.clone.1..sunk.1, s32[]{:T(128)} %constant.40.clone.1..sunk.1) | dynamic-update-slice | bytes 2097156 | tf_op jit(solution)/shard_map/while/body/jit(dynamic_update_index_in_dim)/dynamic_update_slice | solution.py:114
  274.0 7.2 bitcast_add_fusion.5
  281.2 9.3 bitcast_add_fusion.6
  307.4 11.2 %copy.66 = bf16[256,8,2,1408]{3,1,2,0:T(8,128)(2,1)} copy(bf16[256,8,2,1408]{3,2,1,0:T(2,128)(2,1)} %bitcast.147) | data formatting | bytes 23068672
  318.7 15.2 %copy.41 = bf16[2816,2048]{1,0:T(8,128)(2,1)} copy(bf16[2816,2048]{0,1:T(8,128)(2,1)} %bitcast.143) | data formatting | bytes 23068672 | tf_op jit(solution)/shard_map/dot_general | solution.py:116
  333.9 19.1 %fusion.72 = f32[1024,2,1408]{2,0,1:T(8,128)} fusion(bf16[2,1408,2048]{2,1,0:T(8,128)(2,1)} %bitcast.148, bf16[1024,2048]{1,0:T(8,128)(2,1)} %param.15, f32[2048]{0:T(1024)S(1)} %copy-done.26, f32[2048]{0:T(1024)S(1)} %copy-done.22, f32[1024]{0:T(1024)S(1)} %copy-done.20, f32[1024]{0:T(1024)S(1)} %copy-done.18), kind=kOutput, calls=%fused_computation.130 | convolution fusion | flops 11823742976 | bytes 27287552 | tf_op jit(solution)/shard_map/dot_general | solution.py:116
  353.4 17.5 %fusion.59 = (bf16[1024,1,1408]{2,0,1:T(8,128)(2,1)}, bf16[1024,1,1408]{2,0,1:T(8,128)(2,1)}, bf16[1024,1408]{1,0:T(8,128)(2,1)}) fusion(f32[1024,2,1408]{2,0,1:T(8,128)} %fusion.72, bf16[1024,2048]{1,0:T(8,128)(2,1)} %param.25, bf16[1408,2048]{1,0:T(8,128)(2,1)} %param.24), kind=kOutput, calls=%fused_computation.88 | convolution fusion | flops 5927206912 | bytes 30146560 | tf_op jit(solution)/shard_map/to,fo->tf/dot_general | solution.py:138
  371.0 12.0 %fusion.76 = f32[1024,2048]{1,0:T(8,128)} fusion(bf16[1024,1408]{1,0:T(8,128)(2,1)} %get-tuple-element.292, bf16[1408,2048]{1,0:T(8,128)(2,1)} %param.24), kind=kOutput, calls=%fused_computation.132 | convolution fusion | flops 5905580032 | bytes 17039360 | tf_op jit(solution)/shard_map/dot_general | solution.py:127
  383.1 8.9 fusion.69
  392.0 20.3 %bitcast_add_fusion.2 = f32[1024,2048]{1,0:T(8,128)} fusion(f32[1024,2048,1]{1,0,2:T(8,128)} %fusion.69, bf16[2048,2,1408]{2,1,0:T(2,128)(2,1)} %param.23, bf16[1024,1,1408]{2,0,1:T(8,128)(2,1)} %get-tuple-element.291, bf16[1024,1,1408]{2,0,1:T(8,128)(2,1)} %get-tuple-element.290), kind=kOutput, calls=%fused_computation.69 | convolution fusion | flops 11816140800 | bytes 34078720 | tf_op jit(solution)/shard_map/tjf,djf->td/dot_general | solution.py:184
  412.3 9.1 convolution_add_fusion
  421.5 20.7 %fusion.57 = f32[2048,2,1408]{2,0,1:T(8,128)} fusion(bf16[1024,1,1408]{2,0,1:T(8,128)(2,1)} %get-tuple-element.291, bf16[1024,1,1408]{2,0,1:T(8,128)(2,1)} %get-tuple-element.290, bf16[1024,2048]{1,0:T(8,128)(2,1)} %param.15, f32[2048]{0:T(1024)S(1)} %copy-done.26, f32[2048]{0:T(1024)S(1)} %copy-done.22, f32[1024]{0:T(1024)S(1)} %copy-done.20, ...), kind=kOutput, calls=%fused_computation.84 | convolution fusion | flops 11835277312 | bytes 33054720 | tf_op jit(solution)/shard_map/td,tjf->djf/dot_general | solution.py:142
  442.2 7.1 fusion.63
  449.4 13.8 %fusion.77 = f32[1408,2048]{1,0:T(8,128)} fusion(bf16[1024,1408]{1,0:T(8,128)(2,1)} %get-tuple-element.292, bf16[1024,2048]{1,0:T(8,128)(2,1)} %param.25), kind=kOutput, calls=%fused_computation.133 | convolution fusion | flops 5905580032 | bytes 18612224 | tf_op jit(solution)/shard_map/tf,to->fo/dot_general | solution.py:133
  464.6 15.0 %fusion.68 = f32[2048,3,512]{2,0,1:T(8,128)} fusion(bf16[1024,1,512]{2,0,1:T(8,128)(2,1)} %copy.45, bf16[1024,1,512]{2,0,1:T(8,128)(2,1)} %copy.44, bf16[1024,1,512]{2,0,1:T(8,128)(2,1)S(1)} %copy-done.9, bf16[1024,2048]{1,0:T(8,128)(2,1)} %param.15, f32[2048]{0:T(1024)S(1)} %copy-done.26, f32[2048]{0:T(1024)S(1)} %copy-done.22, f32[1024]{0:T(1024)S(1)} %copy-done.20, ...), kind=kOutput, calls=%fused_computation.128 | convolution fusion | flops 6464471040 | bytes 19947520 | tf_op jit(solution)/shard_map/td,tjc->djc/dot_general | solution.py:174
  481.7 504.8 %all-reduce.4.cloned.1.call-done = (f32[1024,2048]{1,0:T(8,128)}, f32[1024,2048]{1,0:T(8,128)}) async-done(((f32[1024,2048]{1,0:T(8,128)}, f32[1024,2048]{1,0:T(8,128)}), (f32[1024,2048]{1,0:T(8,128)}, f32[1024,2048]{1,0:T(8,128)})) %all-reduce.4.cloned.1.call-update) | async-done | bytes 16777232 | tf_op jit(solution)/shard_map/psum | solution.py:130
  993.0 24.9 %all-reduce = (f32[2048]{0:T(1024)}, f32[2048]{0:T(1024)}, f32[3,512]{1,0:T(4,128)}) all-reduce(f32[2048]{0:T(1024)S(1)} %get-tuple-element.231, f32[2048]{0:T(1024)S(1)} %get-tuple-element.234, f32[3,512]{1,0:T(4,128)S(1)} %convert_reduce_fusion.1), channel_id=1, replica_groups=mesh['dp'=8,'mp'=4] {'dp'}, use_global_device_ids=true, to_apply=%region_17.18 | all-reduce | flops 5632 | bytes 45056 | tf_op jit(solution)/shard_map/psum | solution.py:195
  1017.9 13.6 %fusion.47 = (bf16[1024,2048]{1,0:T(8,128)(2,1)}, bf16[1024,2048]{1,0:T(8,128)(2,1)}) fusion(bf16[1024,2048]{1,0:T(8,128)(2,1)} %param.15, bf16[1024,2048]{1,0:T(8,128)(2,1)} %param.25, f32[1024,2048]{1,0:T(8,128)} %get-tuple-element.285, f32[1024]{0:T(1024)S(1)} %broadcast_multiply_fusion, f32[1024]{0:T(1024)S(1)} %broadcast_multiply_fusion.1, ...), kind=kLoop, calls=%fused_computation.65 | loop fusion | flops 27262976 | bytes 33579008 | tf_op jit(solution)/shard_map/convert_element_type | solution.py:194
  (160 shorter events, 113.3 us)
Async XLA Ops:
  8.0 116.2 %copy-start = (bf16[512,2048]{1,0:T(8,128)(2,1)S(1)}, bf16[512,2048]{1,0:T(8,128)(2,1)}, u32[]{:S(2)}) copy-start(bf16[512,2048]{1,0:T(8,128)(2,1)} %param.22) | copy-start | bytes 6291460
  8.0 978.5 %all-reduce.4.cloned.1.call-start = ((), (), s32[]{:S(2)}) async-start(), calls=%async_computation.8 | async-start | bytes 33554432 | tf_op jit(solution)/shard_map/psum | solution.py:130
  11.7 10.1 copy-start.17
  12.9 8.9 copy-start.19
  12.9 8.9 copy-start.21
  12.9 8.9 copy-start.24
  12.9 8.9 copy-start.25
  45.3 78.9 %copy-start.23 = (bf16[1024]{0:T(1024)(128)(2,1)S(1)}, bf16[1024]{0:T(1024)(128)(2,1)}, u32[]{:S(2)}) copy-start(bf16[1024]{0:T(1024)(128)(2,1)} %fusion.65) | copy-start | bytes 6148
  54.3 4.3 copy-start.2
  136.1 9.7 copy-start.4
  170.9 4.8 copy-start.1
  195.3 6.6 copy-start.5
  214.8 9.7 copy-start.4
  249.6 4.8 copy-start.1
  274.0 7.2 copy-start.5
  291.0 5.6 copy-start.14
  291.0 5.6 copy-start.16
  318.7 15.2 %copy-start.18 = (f32[1024]{0:T(1024)S(1)}, f32[1024]{0:T(1024)}, u32[]{:S(2)}) copy-start(f32[1024]{0:T(1024)} %copy-done.17) | copy-start | bytes 12292
  318.7 15.2 %copy-start.20 = (f32[1024]{0:T(1024)S(1)}, f32[1024]{0:T(1024)}, u32[]{:S(2)}) copy-start(f32[1024]{0:T(1024)} %copy-done.19) | copy-start | bytes 12292
  318.7 15.2 %copy-start.22 = (f32[2048]{0:T(1024)S(1)}, f32[2048]{0:T(1024)}, u32[]{:S(2)}) copy-start(f32[2048]{0:T(1024)} %param.18) | copy-start | bytes 24580
  318.7 15.2 %copy-start.26 = (f32[2048]{0:T(1024)S(1)}, f32[2048]{0:T(1024)}, u32[]{:S(2)}) copy-start(f32[2048]{0:T(1024)} %param.19) | copy-start | bytes 24580
  333.8 19.1 %copy-start.7 = (f32[2,512,8,64]{1,0,3,2:T(2,128)S(1)}, f32[2,512,8,64]{1,0,3,2:T(2,128)}, u32[]{:S(2)}) copy-start(f32[2,512,8,64]{1,0,3,2:T(2,128)} %get-tuple-element.131) | copy-start | bytes 6291460
  352.9 30.1 %slice-start = ((s8[6291456]{0:T(1024)(128)(4,1)}), s8[4194304]{0:T(1024)(128)(4,1)S(1)}, s32[]{:S(2)}) async-start(s8[6291456]{0:T(1024)(128)(4,1)} %bitcast.150), calls=%async_computation.9 | async-start | bytes 8388608
  353.4 58.9 %copy-start.6 = (f32[64,8,2,512]{3,1,2,0:T(8,128)}, f32[64,8,2,512]{3,1,2,0:T(8,128)S(1)}, u32[]{:S(2)}) copy-start(f32[64,8,2,512]{3,1,2,0:T(8,128)S(1)} %copy.65) | copy-start | bytes 6291460
  353.4 29.6 %slice-start.1 = ((s8[6291456]{0:T(1024)(128)(4,1)}), s8[2097152]{0:T(1024)(128)(4,1)S(1)}, s32[]{:S(2)}) async-start(s8[6291456]{0:T(1024)(128)(4,1)} %bitcast.150), calls=%async_computation.10 | async-start | bytes 4194304
  371.0 12.1 %copy-start.8 = (bf16[1024,1,512]{2,0,1:T(8,128)(2,1)S(1)}, bf16[1024,1,512]{2,0,1:T(8,128)(2,1)}, u32[]{:S(2)}) copy-start(bf16[1024,1,512]{2,0,1:T(8,128)(2,1)} %copy.43) | copy-start | bytes 3145732
  371.0 12.1 %copy-start.10 = (bf16[1024,1,512]{2,0,1:T(8,128)(2,1)S(1)}, bf16[1024,1,512]{2,0,1:T(8,128)(2,1)}, u32[]{:S(2)}) copy-start(bf16[1024,1,512]{2,0,1:T(8,128)(2,1)} %copy.44) | copy-start | bytes 3145732
  371.0 12.1 %copy-start.11 = (bf16[1024,1,512]{2,0,1:T(8,128)(2,1)S(1)}, bf16[1024,1,512]{2,0,1:T(8,128)(2,1)}, u32[]{:S(2)}) copy-start(bf16[1024,1,512]{2,0,1:T(8,128)(2,1)} %copy.45) | copy-start | bytes 3145732
  421.4 610.1 %reduce-scatter.9.cloned.1.call-start = ((), (), s32[]{:S(2)}) async-start(), calls=%async_computation.6 | async-start | bytes 25952256 | tf_op jit(solution)/shard_map/reduce_scatter | solution.py:179
  442.2 595.0 %reduce-scatter.7.cloned.1.call-start = ((), (), s32[]{:S(2)}) async-start(), calls=%async_computation.5 | async-start | bytes 4718592 | tf_op jit(solution)/shard_map/reduce_scatter | solution.py:178
  449.4 587.8 %reduce-scatter.11.cloned.1.call-start = ((), (), s32[]{:S(2)}) async-start(), calls=%async_computation.7 | async-start | bytes 12976128 | tf_op jit(solution)/shard_map/reduce_scatter | solution.py:180
  463.2 573.9 %reduce-scatter.5.cloned.1.call-start = ((), (), s32[]{:S(2)}) async-start(), calls=%async_computation.4 | async-start | bytes 14155776 | tf_op jit(solution)/shard_map/reduce_scatter | solution.py:177
  (6 other events, 15.5 us)
Sparse Core Ops, SparseCore 0:
  421.5 564.9 all-reduce.3
Sparse Core Ops, SparseCore 1:
  442.2 148.9 reduce-scatter.8
  595.0 50.9 reduce-scatter.6
  649.9 86.7 reduce-scatter.10
  740.7 91.9 reduce-scatter.4
where the time goes:
time: 1060 us; the launch traced here: 1050 us
  waiting for transfers between devices  505 us (48%)
  matrix products  262 us (25%)
  local copies, waits for them, and re-layouts  156 us (15%)
  other arithmetic  71.6 us (7%)
  blocking collectives  24.9 us (2%)
  between operations  17.2 us (2%)
    psum x1, waiting for transfers between devices, shards(): summed = lax.psum(partial_value, 'mp')  505 us
    dynamic_update_slice x8, local copies, waits for them, and re-layouts, shards(): attn_blocks, log_sums = lax.map(forward_block, starts)  86.9 us
    dot_general x4, matrix products, scores(): jnp.einsum('qhd,khd->hqk', part, key, preferred_element_type=jnp.float32)  36.8 us
    unnamed x54, local copies, waits for them, and re-layouts  28.3 us
    psum x1, blocking collectives, shards(): lax.psum((grad_bias, gain_product, shift_part), 'dp')  24.9 us
    convert_element_type x2, other arithmetic, backward_block(): d_score = d_score.astype(jnp.bfloat16)  22.7 us
  transfers between devices with their start and end apart: 5, of which 1 were waited for; matrix products, arithmetic and copies ran while one was open for 8% of the time, Pallas kernels for 0%

commit v1 on v0

v1 whole, which is shorter than its diff:
```python
import functools
import math

import jax
import jax.numpy as jnp
import numpy as np
from jax import lax
from jax.experimental import pallas as pl
from jax.experimental.pallas import tpu as pltpu
from jax.sharding import PartitionSpec as P

HEAD_DIM = 64
ROT = 16
DOCS = 4
DOC_MOST = 512
EPS = 1e-05
BQ = 256
LOG2E = math.log2(math.e)
SCALE2 = HEAD_DIM ** (-0.5) * LOG2E
F32 = jnp.float32
BF16 = jnp.bfloat16
NT = (((1,), (1,)), ((), ()))
TN = (((0,), (0,)), ((), ()))


def dot(a, b, dims=(((1,), (0,)), ((), ()))):
    return lax.dot_general(a, b, dims, preferred_element_type=F32)


def turn(x, cosine, sine):
    lane = lax.broadcasted_iota(jnp.int32, x.shape, 1) % HEAD_DIM
    other = jnp.where(
        lane < ROT // 2, pltpu.roll(x, 128 - ROT // 2, 1), pltpu.roll(x, ROT // 2, 1)
    )
    return x * cosine + other * sine


def head_masks(x):
    low = lax.broadcasted_iota(jnp.int32, x.shape, 1) < HEAD_DIM
    zero = jnp.zeros_like(x)
    return (jnp.where(low, x, zero), jnp.where(low, zero, x))


def key_range(block):
    first = max(0, block - DOC_MOST // BQ)
    return first * BQ, (block + 1) * BQ


def masked_scores(keys, query, first, block, low_row):
    score = dot(keys, query, NT) * SCALE2
    index = first + lax.broadcasted_iota(jnp.int32, score.shape, 0)
    column = block * BQ + lax.broadcasted_iota(jnp.int32, score.shape, 1)
    allowed = (index >= low_row) & (index <= column)
    return score, allowed


def attn_fwd_body(before, q_in, k_in, v_in, bias, cosine, sine, low, valid, *rest):
    if before:
        old_k, old_v, q_out, k_out, v_out, o_out, lse_out, k_all, vt_all = rest
    else:
        q_out, k_out, v_out, o_out, lse_out, k_all, vt_all = rest
    count = q_in.shape[0]
    cos_t, sin_t = cosine[...], sine[...]
    query = turn(q_in[...] + bias[0:1], cos_t, sin_t).astype(BF16)
    key = turn(k_in[...] + bias[1:2], cos_t, sin_t).astype(BF16)
    value = (v_in[...] + bias[2:3]).astype(BF16)
    q_out[...] = query
    k_out[...] = key
    v_out[...] = value
    if before:
        k_all[:before] = old_k[...]
        vt_all[:, :before] = old_v[...].T
    k_all[before:] = key
    vt_all[:, before:] = value.T
    for local in range(count // BQ):
        block = before // BQ + local
        first, last = key_range(block)
        span = slice(local * BQ, (local + 1) * BQ)
        low_row = low[:, span]
        outs = []
        for head, part in enumerate(head_masks(q_out[span])):
            score, allowed = masked_scores(k_all[first:last], part, first, block, low_row)
            score = jnp.where(allowed, score, -1e30)
            top = jnp.max(score, axis=0, keepdims=True)
            expo = jnp.exp2(score - top)
            total = jnp.sum(expo, axis=0, keepdims=True)
            prob = (expo * (1.0 / total)).astype(BF16)
            outs.append(dot(vt_all[:, first:last], prob))
            lse_out[0, head : head + 1, span] = top + jnp.log2(total)
        upper = lax.broadcasted_iota(jnp.int32, outs[0].shape, 0) < HEAD_DIM
        joined = jnp.where(upper, outs[0], outs[1]) * valid[:, span]
        o_out[span] = joined.T.astype(BF16)


def attn_fwd(qkv, bias, cosine, sine, low, valid, old):
    count, local = qkv[0].shape
    before = 0 if old is None else old[0].shape[0]
    pairs = local // 128
    row = lambda n: pl.BlockSpec((n, 128), lambda i: (0, i))
    whole = lambda a: pl.BlockSpec(a.shape, lambda i: (0,) * a.ndim)
    args = list(qkv) + [bias, cosine, sine, low, valid] + ([] if old is None else list(old))
    specs = [row(count)] * 3 + [row(3), whole(cosine), whole(sine), whole(low), whole(valid)]
    specs += [row(before)] * (0 if old is None else 2)
    flat = jax.ShapeDtypeStruct((count, local), BF16)
    return pl.pallas_call(
        functools.partial(attn_fwd_body, before),
        grid=(pairs,),
        in_specs=specs,
        out_specs=[row(count)] * 4 + [pl.BlockSpec((1, 2, count), lambda i: (i, 0, 0))],
        out_shape=[flat] * 4 + [jax.ShapeDtypeStruct((pairs, 2, count), F32)],
        scratch_shapes=[
            pltpu.VMEM((before + count, 128), BF16),
            pltpu.VMEM((128, before + count), BF16),
        ],
        cost_estimate=pl.CostEstimate(
            flops=8 * count * 768 * local, bytes_accessed=20 * count * local, transcendentals=0
        ),
        name="attn_fwd",
    )(*args)


def attn_bwd_body(parts, *refs):
    qs, ks, vs = refs[:parts], refs[parts : 2 * parts], refs[2 * parts : 3 * parts]
    lses = refs[3 * parts : 4 * parts]
    do_in, cosine, sine, low, dq_out, dk_out, dv_out, bias_out, kt_all, dk_acc, dv_acc = refs[
        4 * parts :
    ]
    each = qs[0].shape[0]

    def rows(refs_of, first, last):
        pieces = []
        for part, ref in enumerate(refs_of):
            lo, hi = max(first, part * each), min(last, (part + 1) * each)
            if lo < hi:
                pieces.append(ref[lo - part * each : hi - part * each])
        return pieces[0] if len(pieces) == 1 else jnp.concatenate(pieces, axis=0)

    for part in range(parts):
        kt_all[:, part * each : (part + 1) * each] = ks[part][...].T
    dk_acc[...] = jnp.zeros_like(dk_acc)
    dv_acc[...] = jnp.zeros_like(dv_acc)
    sums = [jnp.zeros((1, 128), F32) for _ in range(3)]
    blocks = parts * each // BQ
    for block in range(blocks):
        first, last = key_range(block)
        span = slice(block * BQ, (block + 1) * BQ)
        low_row = low[:, span]
        part, inside = block * BQ // each, block * BQ % each
        queries = head_masks(rows(qs, span.start, span.stop))
        d_outs = head_masks(do_in[span])
        keys, values = rows(ks, first, last), rows(vs, first, last)
        probs, d_scores, d_queries = [], [], []
        for head in range(2):
            score, allowed = masked_scores(keys, queries[head], first, block, low_row)
            lse = lses[part][0, head : head + 1, inside : inside + BQ]
            prob = jnp.where(allowed, jnp.exp2(score - lse), 0.0)
            d_prob = dot(values, d_outs[head], NT)
            delta = jnp.sum(prob * d_prob, axis=0, keepdims=True)
            d_score = (prob * (d_prob - delta)).astype(BF16)
            probs.append(prob.astype(BF16))
            d_scores.append(d_score)
            d_queries.append(dot(kt_all[:, first:last], d_score))
        wide = slice(first, last)
        dv_acc[wide] += dot(jnp.concatenate(probs, 1), jnp.concatenate(d_outs, 0))
        dk_acc[wide] += dot(jnp.concatenate(d_scores, 1), jnp.concatenate(queries, 0))
        upper = lax.broadcasted_iota(jnp.int32, d_queries[0].shape, 0) < HEAD_DIM
        d_query = jnp.where(upper, d_queries[0], d_queries[1]).T * HEAD_DIM ** (-0.5)
        d_query = turn(d_query, cosine[span], -sine[span]).astype(BF16)
        dq_out[span] = d_query
        sums[0] += jnp.sum(d_query.astype(F32), axis=0, keepdims=True)
        done = [block - DOC_MOST // BQ] if block + 1 < blocks else range(block - DOC_MOST // BQ, blocks)
        for old in done:
            if old < 0:
                continue
            there = slice(old * BQ, (old + 1) * BQ)
            d_key = dk_acc[there] * HEAD_DIM ** (-0.5)
            d_key = turn(d_key, cosine[there], -sine[there]).astype(BF16)
            d_value = dv_acc[there].astype(BF16)
            dk_out[there] = d_key
            dv_out[there] = d_value
            sums[1] += jnp.sum(d_key.astype(F32), axis=0, keepdims=True)
            sums[2] += jnp.sum(d_value.astype(F32), axis=0, keepdims=True)
    bias_out[...] = jnp.concatenate(sums, axis=0)


def attn_bwd(qs, ks, vs, lses, d_out, cosine, sine, low):
    parts = len(qs)
    each, local = qs[0].shape
    count = parts * each
    row = lambda n: pl.BlockSpec((n, 128), lambda i: (0, i))
    whole = lambda a: pl.BlockSpec(a.shape, lambda i: (0,) * a.ndim)
    flat = jax.ShapeDtypeStruct((count, local), BF16)
    return pl.pallas_call(
        functools.partial(attn_bwd_body, parts),
        grid=(local // 128,),
        in_specs=[row(each)] * (3 * parts)
        + [pl.BlockSpec((1, 2, each), lambda i: (i, 0, 0))] * parts
        + [row(count), whole(cosine), whole(sine), whole(low)],
        out_specs=[row(count)] * 3 + [row(3)],
        out_shape=[flat] * 3 + [jax.ShapeDtypeStruct((3, local), F32)],
        scratch_shapes=[
            pltpu.VMEM((128, count), BF16),
            pltpu.VMEM((count, 128), F32),
            pltpu.VMEM((count, 128), F32),
        ],
        cost_estimate=pl.CostEstimate(
            flops=20 * count * 768 * local, bytes_accessed=20 * count * local, transcendentals=0
        ),
        name="attn_bwd",
    )(*qs, *ks, *vs, *lses, d_out, cosine, sine, low)


def mlp_body(x_in, dy_in, w_in, down_in, h_out, dg_out, du_out):
    for start in range(0, x_in.shape[0], 256):
        span = slice(start, start + 256)
        gate = dot(x_in[span], w_in[0])
        upper = dot(x_in[span], w_in[1])
        d_hidden = dot(dy_in[span], down_in[...], NT)
        sigma = jax.nn.sigmoid(gate)
        active = gate * sigma
        h_out[span] = (active * upper).astype(BF16)
        du_out[span] = (d_hidden * active).astype(BF16)
        dg_out[span] = (d_hidden * upper * sigma * (1.0 + gate * (1.0 - sigma))).astype(BF16)


def mlp(normed, y_grad, weight, down, part, parts):
    count, width = normed.shape
    rows = count // parts
    hidden = down.shape[0]
    step = min(256, hidden)
    fixed = pl.BlockSpec((rows, width), lambda i: (part, 0))
    return pl.pallas_call(
        mlp_body,
        grid=(pl.cdiv(hidden, step),),
        in_specs=[
            fixed,
            fixed,
            pl.BlockSpec((2, width, step), lambda i: (0, 0, i)),
            pl.BlockSpec((step, width), lambda i: (i, 0)),
        ],
        out_specs=[pl.BlockSpec((rows, step), lambda i: (0, i))] * 3,
        out_shape=[jax.ShapeDtypeStruct((rows, hidden), BF16)] * 3,
        cost_estimate=pl.CostEstimate(
            flops=6 * rows * width * hidden, bytes_accessed=6 * width * hidden, transcendentals=0
        ),
        name="mlp",
    )(normed, y_grad, weight, down)


def out_body(o_in, h_in, wo_in, wd_in, out):
    out[...] = (dot(o_in[...], wo_in[...]) + dot(h_in[...], wd_in[...])).astype(BF16)


def out_partial(o, h, out_weight, down, start, cols):
    rows, local = o.shape
    hidden = h.shape[1]
    step = min(512, cols)
    base = start // step
    return pl.pallas_call(
        out_body,
        grid=(cols // step,),
        in_specs=[
            pl.BlockSpec((rows, local), lambda i: (0, 0)),
            pl.BlockSpec((rows, hidden), lambda i: (0, 0)),
            pl.BlockSpec((local, step), lambda i: (0, base + i)),
            pl.BlockSpec((hidden, step), lambda i: (0, base + i)),
        ],
        out_specs=pl.BlockSpec((rows, step), lambda i: (0, i)),
        out_shape=jax.ShapeDtypeStruct((rows, cols), BF16),
        cost_estimate=pl.CostEstimate(
            flops=2 * rows * cols * (local + hidden),
            bytes_accessed=2 * (rows + cols) * (local + hidden),
            transcendentals=0,
        ),
        name="out_partial",
    )(o, h, out_weight, down)


def dxn_body(parts, bounds, *refs):
    dq_in, dk_in, dv_in = refs[:3]
    dgs, dus = refs[3 : 3 + parts], refs[3 + parts : 3 + 2 * parts]
    wqkv_in, w_in, x_in, mean_in, inv_in, gain_in, *outs, col_out, r1_out, r2_out = refs[
        3 + 2 * parts :
    ]
    step = pl.program_id(0)
    count = x_in.shape[0]
    each = count // parts
    first = pl.program_id(0) == 0
    gain = gain_in[...]
    shift_sum = jnp.zeros(gain.shape, F32)
    gain_sum = jnp.zeros(gain.shape, F32)
    for start in range(0, count, 256):
        span = slice(start, start + 256)
        part = start // each
        inside = slice(start - part * each, start - part * each + 256)
        total = dot(dq_in[span], wqkv_in[0], NT)
        total += dot(dk_in[span], wqkv_in[1], NT)
        total += dot(dv_in[span], wqkv_in[2], NT)
        total += dot(dgs[part][inside], w_in[0], NT)
        total += dot(dus[part][inside], w_in[1], NT)
        for out, (low, high) in zip(outs, bounds):

            @pl.when((step >= low) & (step < high))
            def _(out=out, span=span, total=total):
                out[span] = total.astype(BF16)

        hat = (x_in[span].astype(F32) - mean_in[span]) * inv_in[span]
        product = total * hat
        shift_sum += jnp.sum(total, axis=0, keepdims=True)
        gain_sum += jnp.sum(product, axis=0, keepdims=True)
        row1 = jnp.sum(total * gain, axis=1, keepdims=True)
        row2 = jnp.sum(product * gain, axis=1, keepdims=True)
        r1_out[span] = row1 + jnp.where(first, 0.0, r1_out[span])
        r2_out[span] = row2 + jnp.where(first, 0.0, r2_out[span])
    col_out[...] = jnp.concatenate([gain_sum, shift_sum], axis=0)


def dxn_partial(dqkv, dgs, dus, wqkv, weight, x, mean, inv, gain, start, widths):
    parts = len(dgs)
    cols = sum(widths)
    count = x.shape[0]
    local, hidden = dqkv[0].shape[1], dgs[0].shape[1]
    each = count // parts
    step = 256
    base = start // step
    ends = np.cumsum([w // step for w in widths])
    bounds = [(int(e) - w // step, int(e)) for e, w in zip(ends, widths)]
    whole = lambda a: pl.BlockSpec(a.shape, lambda i: (0,) * a.ndim)
    return pl.pallas_call(
        functools.partial(dxn_body, parts, bounds),
        grid=(cols // step,),
        in_specs=[whole(a) for a in (*dqkv, *dgs, *dus)]
        + [
            pl.BlockSpec((3, step, local), lambda i: (0, base + i, 0)),
            pl.BlockSpec((2, step, hidden), lambda i: (0, base + i, 0)),
            pl.BlockSpec((count, step), lambda i: (0, base + i)),
            whole(mean),
            whole(inv),
            pl.BlockSpec((1, step), lambda i: (0, base + i)),
        ],
        out_specs=[
            pl.BlockSpec((count, step), lambda i, b=b: (0, jnp.clip(i - b[0], 0, b[1] - b[0] - 1)))
            for b in bounds
        ]
        + [
            pl.BlockSpec((2, step), lambda i: (0, i)),
            pl.BlockSpec((count, 1), lambda i: (0, 0)),
            pl.BlockSpec((count, 1), lambda i: (0, 0)),
        ],
        out_shape=[
            *(jax.ShapeDtypeStruct((count, w), BF16) for w in widths),
            jax.ShapeDtypeStruct((2, cols), F32),
            jax.ShapeDtypeStruct((count, 1), F32),
            jax.ShapeDtypeStruct((count, 1), F32),
        ],
        cost_estimate=pl.CostEstimate(
            flops=2 * count * cols * (3 * local + 2 * hidden),
            bytes_accessed=2 * (count + cols) * (3 * local + 2 * hidden),
            transcendentals=0,
        ),
        name="dxn_partial",
    )(*dqkv, *dgs, *dus, wqkv, weight, x, mean, inv, gain)


def dw_sum(groups, lhs, rhs):
    position = 0
    for parts in groups:
        each = lhs.shape[0] // parts
        total = None
        for part in range(parts):
            piece = dot(lhs[part * each : (part + 1) * each], rhs[position][...], TN)
            total = piece if total is None else total + piece
            position += 1
        yield total


def dw_send_body(groups, order, lhs, *refs):
    rhs, outs = refs[: sum(groups)], refs[sum(groups) :]
    for total, out in zip(dw_sum(groups, lhs, rhs), outs):
        out[0] = total.astype(BF16)


def dw_keep_body(groups, order, slots, lhs, *refs):
    rhs, refs = refs[: sum(groups)], refs[sum(groups) :]
    number = len(groups)
    received, sends, keeps = refs[:number], refs[number : 2 * number], refs[2 * number :]
    step = pl.program_id(0)
    for group, total in enumerate(dw_sum(groups, lhs, rhs)):
        total = (total + received[group][0].astype(F32)).astype(BF16)
        away = slots[3 * group, step] == 1

        @pl.when(away)
        def _(group=group, total=total):
            sends[group][0] = total

        @pl.when(jnp.logical_not(away))
        def _(group=group, total=total):
            keeps[group][0] = total


def dw_call(order, lhs, rhs, number, received=None, slots=None):
    count, width = lhs.shape
    step = width // (2 * number)
    groups = tuple(len(group) for group in rhs)
    flat = [part for group in rhs for part in group]
    columns = [group[0].shape[1] for group in rhs]
    scalars = [order] if slots is None else [order, slots]
    args = scalars + [lhs, *flat]
    specs = [pl.BlockSpec((count, step), lambda i, order, *_: (0, order[i]))]
    specs += [pl.BlockSpec(a.shape, lambda i, *_: (0, 0)) for a in flat]
    if received is None:
        body = functools.partial(dw_send_body, groups)
        out_specs = [pl.BlockSpec((1, step, c), lambda i, *_: (i, 0, 0)) for c in columns]
        shapes = [jax.ShapeDtypeStruct((number, step, c), BF16) for c in columns]
    else:
        body = functools.partial(dw_keep_body, groups)
        args += received
        specs += [pl.BlockSpec((1, step, c), lambda i, *_: (i, 0, 0)) for c in columns]
        out_specs = [
            pl.BlockSpec((1, step, c), lambda i, order, slots, r=3 * g + kind: (slots[r, i], 0, 0))
            for kind in (1, 2)
            for g, c in enumerate(columns)
        ]
        shapes = [jax.ShapeDtypeStruct((number // 2, step, c), BF16) for c in columns] * 2
    total = number * step * sum(columns)
    return pl.pallas_call(
        body,
        grid_spec=pltpu.PrefetchScalarGridSpec(
            num_scalar_prefetch=len(scalars), grid=(number,), in_specs=specs, out_specs=out_specs
        ),
        out_shape=shapes,
        cost_estimate=pl.CostEstimate(
            flops=2 * count * total, bytes_accessed=2 * (count * sum(columns) + total), transcendentals=0
        ),
        name="weight_grad",
    )(*args)


def flip(size, bit):
    return [(i, i ^ bit) for i in range(size)]


class Order:
    def __init__(self):
        self.token = None

    def __call__(self, function, *args):
        if self.token is not None:
            args, _ = lax.optimization_barrier((args, self.token))
        out = function(*args)
        self.token = jax.tree.leaves(out)[0]
        return out


def halving_order(bits):
    order = [0]
    for bit in reversed(bits):
        order = [offset ^ bit for offset in order] + order
    return order


class Scatter:
    def __init__(self, run, devices, lhs, rhs, swaps):
        self.run, self.devices, self.lhs, self.rhs = run, devices, lhs, rhs
        bits = [1 << i for i in range(devices.bit_length() - 1)]
        self.offsets = halving_order(bits)
        self.order = lax.axis_index("dp").astype(jnp.int32) ^ jnp.asarray(self.offsets, jnp.int32)
        self.bits = []
        for swap in swaps:
            rest = bits[1:]
            if swap and len(rest) > 1:
                rest[0], rest[1] = rest[1], rest[0]
            self.bits.append(rest)

    def send(self):
        half = self.devices // 2
        call = lambda lhs, rhs: dw_call(self.order[:half], lhs, rhs, half)
        sent = self.run(call, self.lhs, self.rhs)
        self.received = [lax.ppermute(s, "dp", flip(self.devices, 1)) for s in sent]

    def keep(self):
        half = self.devices // 2
        kept = self.offsets[half:]
        rows, self.left = [], []
        for bits in self.bits:
            away = [int(offset & bits[0] != 0) for offset in kept]
            place = lambda flags: [max(0, sum(flags[: i + 1]) - 1) for i in range(half)]
            rows += [away, place(away), place([1 - a for a in away])]
            self.left.append([offset for offset in kept if not offset & bits[0]])
        slots = jnp.asarray(np.array(rows), jnp.int32)
        call = lambda lhs, rhs, received: dw_call(self.order[half:], lhs, rhs, half, received, slots)
        outs = self.run(call, self.lhs, self.rhs, self.received)
        number = len(self.bits)
        self.kept = outs[number:]
        self.received = [
            lax.ppermute(s, "dp", flip(self.devices, bits[0])) for s, bits in zip(outs, self.bits)
        ]
        self.stage = 1

    def next(self):
        def step(kept, received):
            sends, keeps = [], []
            for group, bits in enumerate(self.bits):
                bit = bits[self.stage]
                for away, stack in ((True, sends), (False, keeps)):
                    where = [i for i, o in enumerate(self.left[group]) if bool(o & bit) == away]
                    pick = lambda a: jnp.stack([a[i] for i in where]).astype(F32)
                    stack.append((pick(kept[group]) + pick(received[group])).astype(BF16))
            return sends, keeps

        sends, self.kept = self.run(step, self.kept, self.received)
        self.received = []
        for group, bits in enumerate(self.bits):
            bit = bits[self.stage]
            self.left[group] = [o for o in self.left[group] if not o & bit]
            self.received.append(lax.ppermute(sends[group], "dp", flip(self.devices, bit)))
        self.stage += 1

    def last(self, shape=lambda a: a):
        while self.stage < len(self.bits[0]):
            self.next()
        add = lambda kept, received: shape(
            [k[0].astype(F32) + r[0].astype(F32) for k, r in zip(kept, received)]
        )
        return self.run(add, self.kept, self.received)


LINE = 4


class Line:
    def __init__(self, run, size, partial, finish, corner):
        self.run, self.size, self.partial, self.finish, self.corner = run, size, partial, finish, corner
        lines = range(0, size, LINE)
        inward = [(b, b + 1) for b in lines] + [(b + 3, b + 2) for b in lines]
        self.across = [(b + 1, b + 2) for b in lines] + [(b + 2, b + 1) for b in lines]
        self.outward = [(b + 1, b) for b in lines] + [(b + 2, b + 3) for b in lines]
        self.received = lax.ppermute(partial, "mp", inward)

    def mid(self):
        add = lambda a, b: (a.astype(F32) + b.astype(F32)).astype(BF16)
        self.total = self.run(add, self.partial, self.received)
        self.received = lax.ppermute(self.total, "mp", self.across)

    def back(self):
        def step(total, received):
            total = total.astype(F32) + received.astype(F32)
            bit = LINE
            while bit < self.size:
                total = total.astype(BF16)
                pairs = [(i, i ^ bit) for i in range(self.size) if i % LINE in (1, 2)]
                total = total.astype(F32) + lax.ppermute(total, "mp", pairs).astype(F32)
                bit *= 2
            return self.finish(total)

        self.mine = self.run(step, self.total, self.received)
        self.received = lax.ppermute(self.mine, "mp", self.outward)

    def store(self, target):
        place = lax.axis_index("mp") % LINE
        inner = (place == 1) | (place == 2)
        step = lambda target, mine, received: lax.dynamic_update_slice(
            target, jnp.where(inner, mine, received), self.corner
        )
        return self.run(step, target, self.mine, self.received)


def small_sum(value, axis, size):
    bit = 1
    while bit < size:
        value = value + lax.ppermute(value, axis, flip(size, bit))
        bit *= 2
    return value


def shards(
    dp,
    mp,
    inputs,
    segment_ids,
    pad_count,
    layer_norm_gain,
    layer_norm_bias,
    qkv_weight,
    qkv_bias,
    out_weight,
    gateup_weight,
    down_weight,
    y_grad,
):
    count, width = inputs.shape
    local = qkv_weight.shape[2]
    parts = 2
    rows = count // parts

    seg = segment_ids[0]
    steps = jnp.arange(count, dtype=jnp.int32)
    start = jnp.sum((seg[None, :] < seg[:, None]).astype(jnp.int32), axis=1)
    valid = steps < count - pad_count[0]
    low = jnp.where(valid, start, steps)[None, :]
    valid_row = valid.astype(F32)[None, :]
    lane = jnp.arange(128, dtype=jnp.int32) % HEAD_DIM
    half = ROT // 2
    freq = jnp.power(10000.0, -2.0 * (lane % half).astype(F32) / ROT)
    freq = jnp.where(lane < ROT, freq, 0.0)
    angle = (steps - start).astype(F32)[:, None] * freq[None, :]
    sign = jnp.where(lane < half, -1.0, 1.0)
    cosine = jnp.cos(angle)
    sine = jnp.sin(angle) * sign[None, :]

    xf = inputs.astype(F32)
    mean = jnp.mean(xf, axis=-1, keepdims=True)
    removed = xf - mean
    inv = lax.rsqrt(jnp.mean(removed * removed, axis=-1, keepdims=True) + EPS)
    normed = (removed * inv * layer_norm_gain + layer_norm_bias).astype(BF16)

    wqkv = jnp.transpose(qkv_weight, (1, 0, 2))
    weight = jnp.transpose(gateup_weight, (1, 0, 2))

    run = Order()
    old = None
    qs, ks, vs, os, lses, hs, dgs, dus = ([] for _ in range(8))
    firsts = []
    for part in range(parts):
        span = slice(part * rows, (part + 1) * rows)

        def attend(normed, old, span=span):
            xs = normed[span]
            qkv = [jnp.dot(xs, wqkv[j], preferred_element_type=F32) for j in range(3)]
            return attn_fwd(
                qkv, qkv_bias, cosine[span], sine[span], low[:, span], valid_row[:, span], old
            )

        q, k, v, o, lse = run(attend, normed, old)
        old = (k, v)
        h, dg, du = run(
            lambda *a, part=part: mlp(*a, part, parts), normed, y_grad, weight, down_weight
        )
        for stack, item in zip((qs, ks, vs, os, lses, hs, dgs, dus), (q, k, v, o, lse, h, dg, du)):
            stack.append(item)
        partial = run(lambda *a: out_partial(*a, 0, width), o, h, out_weight, down_weight)
        x_here = inputs[span].astype(F32)
        finish = lambda total, x_here=x_here: (x_here + total).astype(BF16)
        firsts.append(Line(run, mp, partial, finish, (part * rows, 0)))
    result = jnp.zeros((count, width), BF16)
    x_grad = jnp.zeros((count, width), BF16)

    gateup = Scatter(run, dp, normed, [dgs, dus], (False, True))
    down = Scatter(run, dp, y_grad, [hs], (True,))
    outer = Scatter(run, dp, y_grad, [os], (True,))

    firsts[0].mid()
    gateup.send()

    def cotangent(y_grad, out_weight):
        d_attn = lax.dot_general(y_grad, out_weight, NT, preferred_element_type=F32).astype(BF16)
        return d_attn * valid.astype(BF16)[:, None]

    d_attn = run(cotangent, y_grad, out_weight)
    gateup.keep()
    *dqkv, bias_grad = run(
        lambda *a: attn_bwd(*a, cosine, sine, low), qs, ks, vs, lses, d_attn
    )
    inner = Scatter(run, dp, normed, [[a] for a in dqkv], (False, False, False))

    gain_row = layer_norm_gain[None, :]
    averages = []
    seconds = []
    sums = []

    def finish(total, span):
        average, slope = averages[0]
        hat = (inputs[:, span].astype(F32) - mean) * inv
        inner = total * layer_norm_gain[span] - average - hat * slope
        return (y_grad[:, span].astype(F32) + inv * inner).astype(BF16)

    def emit(start, widths):
        call = lambda dqkv, dgs, dus: dxn_partial(
            dqkv, dgs, dus, wqkv, weight, inputs, mean, inv, gain_row, start, widths
        )
        *chunks, column, row1, row2 = run(call, dqkv, dgs, dus)
        sums.append((column, row1, row2))
        for chunk, cols in zip(chunks, widths):
            span = slice(start, start + cols)
            seconds.append(
                Line(run, mp, chunk, functools.partial(finish, span=span), (0, start))
            )
            start += cols

    emit(0, (512, 512))
    firsts[1].mid()
    firsts[0].back()
    emit(1024, (512, 512))

    def gather(sums):
        columns = jnp.concatenate([c[0] for c in sums], axis=1)
        row1 = sum(c[1] for c in sums).reshape(count)
        row2 = sum(c[2] for c in sums).reshape(count)
        return jnp.concatenate([row1, row2, columns.reshape(2 * width)])

    small = small_sum(run(gather, sums), "mp", mp)
    gateup.next()
    down.send()
    average = (small[:count] / width).reshape(count, 1)
    slope = (small[count : 2 * count] / width).reshape(count, 1)
    averages.append((average, slope))
    small = jnp.concatenate([small[2 * count :], bias_grad.reshape(-1)])
    seconds[0].mid()
    outer.send()
    down.keep()
    outer.keep()
    seconds[1].mid()
    firsts[1].back()
    result = firsts[0].store(result)
    inner.send()
    seconds[0].back()
    inner.keep()
    seconds[2].mid()
    flat = lambda a: jnp.transpose(a[0])
    gateup_grad = gateup.last(lambda a: jnp.stack(a, axis=1))
    down.next()
    seconds[1].back()
    outer.next()
    x_grad = seconds[0].store(x_grad)
    result = firsts[1].store(result)
    seconds[3].mid()
    inner.next()
    small = small_sum(small, "dp", dp)
    column_sums = small[: 2 * width].reshape(2, width)
    bias_sum = small[2 * width :].reshape(bias_grad.shape)
    down_grad = down.last(flat)
    seconds[2].back()
    x_grad = seconds[1].store(x_grad)
    out_grad = outer.last(flat)
    qkv_grad = inner.last(lambda a: jnp.transpose(jnp.stack(a), (1, 0, 2)))
    seconds[3].back()
    x_grad = seconds[2].store(x_grad)
    x_grad = seconds[3].store(x_grad)
    return (
        result,
        x_grad,
        column_sums[0],
        column_sums[1],
        qkv_grad,
        bias_sum,
        out_grad,
        gateup_grad,
        down_grad,
    )


def solution(mesh):
    placed = (
        P("dp", None),
        P("dp", None),
        P("dp"),
        P(),
        P(),
        P(None, None, "mp"),
        P(None, "mp"),
        P("mp", None),
        P(None, None, "mp"),
        P("mp", None),
        P("dp", None),
    )
    return jax.shard_map(
        functools.partial(shards, mesh.shape["dp"], mesh.shape["mp"]),
        mesh=mesh,
        in_specs=placed,
        out_specs=(
            P("dp", None),
            P("dp", None),
            P(),
            P(),
            P("dp", None, "mp"),
            P(None, "mp"),
            P("mp", "dp"),
            P("dp", None, "mp"),
            P("mp", "dp"),
        ),
        check_vma=False,
    )
```

time: 1060 us -> 580 us (0.55)
  waiting for transfers between devices: 505 us -> 149 us
  matrix products: 262 us -> 25.1 us
  Pallas kernels: 0 us -> 229 us
  local copies, waits for them, and re-layouts: 156 us -> 26.7 us
  starting transfers between devices: 0.21 us -> 61.9 us
  blocking collectives: 24.9 us -> 0 us
  between operations: 17.2 us -> 2.6 us
    psum x1 -> x0, waiting for transfers between devices: 505 us -> none  [shards(): summed = lax.psum(partial_value, 'mp')]
    dot_general x26 -> x7, matrix products: 262 us -> 25.1 us  [the longest x6 18.9 us: attend(): qkv = [jnp.dot(xs, wqkv[j], preferred_element_type=F32) for j in range(3)]]
    pallas_call x0 -> x17, Pallas kernels: none -> 229 us  [the longest x8 74 us: dw_call(): pl.pallas_call(body, grid_spec=pltpu.PrefetchScalarGridSpec(num_scalar_pr...]
    ppermute x0 -> x44, waiting for transfers between devices: none -> 149 us  [the longest x6 57.2 us: back(): self.received = lax.ppermute(self.mine, 'mp', self.outward)]
    dynamic_update_slice x8 -> x0, local copies, waits for them, and re-layouts: 86.9 us -> none  [shards(): attn_blocks, log_sums = lax.map(forward_block, starts)]
    ppermute x0 -> x44, starting transfers between devices: none -> 61.9 us  [the longest x6 25.7 us: __init__(): self.received = lax.ppermute(partial, 'mp', inward)]
    psum x1 -> x0, blocking collectives: 24.9 us -> none  [shards(): lax.psum((grad_bias, gain_product, shift_part), 'dp')]
    reduce_sum x8 -> x3, other arithmetic: 21.4 us -> 4.74 us  [the longest x1 2.95 us: shards(): mean = jnp.mean(xf, axis=-1, keepdims=True)]
  transfers between devices with their start and end apart: 5 -> 44, of which waited for: 1 -> 15; matrix products, arithmetic and copies ran while one was open for 8% -> 16% of each run, Pallas kernels for 0% -> 31%
where the time goes in v1:
time: 580 us; the launch traced here: 569 us
  Pallas kernels  229 us (39%)
  waiting for transfers between devices  149 us (26%)
  other arithmetic  74.4 us (13%)
  starting transfers between devices  61.9 us (11%)
  local copies, waits for them, and re-layouts  26.7 us (5%)
  matrix products  25.1 us (4%)
    pallas_call x8, Pallas kernels, dw_call(): pl.pallas_call(body, grid_spec=pltpu.PrefetchScalarGridSpec(num_scalar_pr...  74 us
    pallas_call x2, Pallas kernels, dxn_partial(): pl.pallas_call(functools.partial(dxn_body, parts, bounds), grid=(cols //...  59.2 us
    ppermute x6, waiting for transfers between devices, back(): self.received = lax.ppermute(self.mine, 'mp', self.outward)  57.2 us
    ppermute x7, waiting for transfers between devices, keep(): lax.ppermute(s, 'dp', flip(self.devices, bits[0]))  41.2 us
    pallas_call x2, Pallas kernels, mlp(): pl.pallas_call(mlp_body, grid=(pl.cdiv(hidden, step),), in_specs=[fixed,...  31.7 us
    ppermute x6, waiting for transfers between devices, __init__(): self.received = lax.ppermute(partial, 'mp', inward)  27.2 us
    ppermute x6, starting transfers between devices, __init__(): self.received = lax.ppermute(partial, 'mp', inward)  25.7 us
    pallas_call x2, Pallas kernels, attn_fwd(): pl.pallas_call(functools.partial(attn_fwd_body, before), grid=(pairs,), i...  24.4 us
  transfers between devices with their start and end apart: 44, of which 15 were waited for; matrix products, arithmetic and copies ran while one was open for 16% of the time, Pallas kernels for 31%

profile of v1, /device:TPU:0, one launch (start us, length us, event | category | flops | bytes accessed | tf_op | source)
XLA Modules:
  0.0 569.3 jit_solution(3297724560564192803)
XLA Ops:
  20.1 6.4 %copy.50 = bf16[2048,2,1408]{2,0,1:T(8,128)(2,1)} copy(bf16[2048,2,1408]{2,1,0:T(2,128)(2,1)S(1)} %bitcast.42) | data formatting | bytes 23068672 | tf_op args[8]
  26.6 10.2 %attn_fwd.2 = (bf16[512,512]{1,0:T(8,128)(2,1)}, bf16[512,512]{1,0:T(8,128)(2,1)}, bf16[512,512]{1,0:T(8,128)(2,1)}, bf16[512,512]{1,0:T(8,128)(2,1)}, f32[4,2,512]{2,1,0:T(2,128)}) custom-call(f32[512,512]{1,0:T(8,128)} %fusion.7.q_in, f32[512,512]{1,0:T(8,128)} %fusion.9.k_in, f32[512,512]{1,0:T(8,128)} %fusion.11.v_in, f32[3,512]{1,0:T(4,128)} %bias.3, ...), custom_call_target="tpu_custom_call" | custom-call | flops 1610612736 | bytes 5242880 | tf_op jit(solution)/shard_map/attn_fwd/pallas_call | solution.py:105
  36.8 15.8 %mlp.2 = (bf16[512,1408]{1,0:T(8,128)(2,1)}, bf16[512,1408]{1,0:T(8,128)(2,1)}, bf16[512,1408]{1,0:T(8,128)(2,1)}) custom-call(bf16[1024,2048]{1,0:T(8,128)(2,1)} %copy-done.6, bf16[1024,2048]{1,0:T(8,128)(2,1)} %lhs.5, bf16[2,2048,1408]{2,1,0:T(8,128)(2,1)} %bitcast.43, bf16[1408,2048]{1,0:T(8,128)(2,1)} %wd_in.1), custom_call_target="tpu_custom_call" | custom-call | flops 8858370048 | bytes 17301504 | tf_op jit(solution)/shard_map/mlp/pallas_call | solution.py:232
  52.6 8.5 %out_partial.2 = bf16[512,2048]{1,0:T(8,128)(2,1)} custom-call(bf16[512,512]{1,0:T(8,128)(2,1)} %get-tuple-element.333.o_in.refs_0_, bf16[512,1408]{1,0:T(8,128)(2,1)} %get-tuple-element.328.h_in.refs_0_, bf16[512,2048]{1,0:T(8,128)(2,1)} %wo_in.1, bf16[1408,2048]{1,0:T(8,128)(2,1)} %wd_in.1), custom_call_target="tpu_custom_call" | custom-call | flops 4026531840 | bytes 9830400 | tf_op jit(solution)/shard_map/out_partial/pallas_call | solution.py:259
  61.1 6.5 %collective-permute-start = (bf16[512,2048]{1,0:T(8,128)(2,1)}, bf16[512,2048]{1,0:T(8,128)(2,1)}, u32[]{:S(2)}, u32[]{:S(2)}) collective-permute-start(bf16[512,2048]{1,0:T(8,128)(2,1)} %out_partial.2), channel_id=1, source_target_pairs={{0,1},{3,2},{4,5},{7,6},{8,9},{11,10},{12,13},{15,14},{16,17},{19,... | collective-permute-start | bytes 6291464 | tf_op jit(solution)/shard_map/ppermute | solution.py:538
  79.9 14.1 %attn_fwd.3 = (bf16[512,512]{1,0:T(8,128)(2,1)}, bf16[512,512]{1,0:T(8,128)(2,1)}, bf16[512,512]{1,0:T(8,128)(2,1)}, bf16[512,512]{1,0:T(8,128)(2,1)}, f32[4,2,512]{2,1,0:T(2,128)}) custom-call(f32[512,512]{1,0:T(8,128)} %fusion.6.q_in, f32[512,512]{1,0:T(8,128)} %fusion.8.k_in, f32[512,512]{1,0:T(8,128)} %fusion.10.v_in, f32[3,512]{1,0:T(4,128)} %bias.3, ...), custom_call_target="tpu_custom_call" | custom-call | flops 1610612736 | bytes 5242880 | tf_op jit(solution)/shard_map/attn_fwd/pallas_call | solution.py:105
  94.0 15.8 %mlp.3 = (bf16[512,1408]{1,0:T(8,128)(2,1)}, bf16[512,1408]{1,0:T(8,128)(2,1)}, bf16[512,1408]{1,0:T(8,128)(2,1)}) custom-call(bf16[1024,2048]{1,0:T(8,128)(2,1)} %copy-done.6, bf16[1024,2048]{1,0:T(8,128)(2,1)} %lhs.5, bf16[2,2048,1408]{2,1,0:T(8,128)(2,1)} %bitcast.44, bf16[1408,2048]{1,0:T(8,128)(2,1)} %wd_in.1), custom_call_target="tpu_custom_call" | custom-call | flops 8858370048 | bytes 17301504 | tf_op jit(solution)/shard_map/mlp/pallas_call | solution.py:232
  110.5 8.7 %out_partial.3 = bf16[512,2048]{1,0:T(8,128)(2,1)} custom-call(bf16[512,512]{1,0:T(8,128)(2,1)} %get-tuple-element.334.o_in.refs_1_, bf16[512,1408]{1,0:T(8,128)(2,1)} %get-tuple-element.329.h_in.refs_1_, bf16[512,2048]{1,0:T(8,128)(2,1)} %wo_in.1, bf16[1408,2048]{1,0:T(8,128)(2,1)} %wd_in.1), custom_call_target="tpu_custom_call" | custom-call | flops 4026531840 | bytes 9830400 | tf_op jit(solution)/shard_map/out_partial/pallas_call | solution.py:259
  122.9 11.9 %weight_grad.8 = (bf16[4,256,1408]{2,1,0:T(8,128)(2,1)}, bf16[4,256,1408]{2,1,0:T(8,128)(2,1)}) custom-call(s32[4]{0:T(128)} %get-tuple-element.481.order, bf16[1024,2048]{1,0:T(8,128)(2,1)} %copy-done.6, bf16[512,1408]{1,0:T(8,128)(2,1)} %get-tuple-element.303.refs_0_.refs_3_, bf16[512,1408]{1,0:T(8,128)(2,1)} %get-tuple-element.304.refs_1_.refs_4_, ...), custom_call_target="tpu_custom_call" | custom-call | flops 5905580032 | bytes 11534336 | tf_op jit(solution)/shard_map/weight_grad/pallas_call | solution.py:426
  142.1 6.2 %fusion.18.refs_8_ = bf16[1024,512]{1,0:T(8,128)(2,1)} fusion(bf16[1024,2048]{1,0:T(8,128)(2,1)} %lhs.5, bf16[512,2048]{1,0:T(8,128)(2,1)} %wo_in.1, bf16[1024]{0:T(1024)(128)(2,1)S(1)} %fusion.20), kind=kOutput, calls=%fused_computation.51 | convolution fusion | flops 2148532224 | bytes 7342080 | tf_op jit(solution)/shard_map/dot_general | solution.py:656
  148.3 15.2 %weight_grad.9 = (bf16[2,256,1408]{2,1,0:T(8,128)(2,1)}, bf16[2,256,1408]{2,1,0:T(8,128)(2,1)}, bf16[2,256,1408]{2,1,0:T(8,128)(2,1)}, bf16[2,256,1408]{2,1,0:T(8,128)(2,1)}) custom-call(s32[4]{0:T(128)} %get-tuple-element.480.order, s32[6,4]{1,0:T(8,128)} %constant.107.clone.slots, bf16[1024,2048]{1,0:T(8,128)(2,1)} %copy-done.6, ...), custom_call_target="tpu_custom_call" | custom-call | flops 5905580032 | bytes 11534336 | tf_op jit(solution)/shard_map/weight_grad/pallas_call | solution.py:426
  164.9 23.0 %attn_bwd.1 = (bf16[1024,512]{1,0:T(8,128)(2,1)}, bf16[1024,512]{1,0:T(8,128)(2,1)}, bf16[1024,512]{1,0:T(8,128)(2,1)}, f32[3,512]{1,0:T(4,128)}) custom-call(bf16[512,512]{1,0:T(8,128)(2,1)} %get-tuple-element.269.refs_0_, bf16[512,512]{1,0:T(8,128)(2,1)} %get-tuple-element.270.refs_1_, bf16[512,512]{1,0:T(8,128)(2,1)} %get-tuple-element.271.rest_0_.refs_2_, ...), custom_call_target="tpu_custom_call" | custom-call | flops 8053063680 | bytes 10485760 | tf_op jit(solution)/shard_map/attn_bwd/pallas_call | solution.py:193
  187.9 29.6 %dxn_partial.2 = (bf16[1024,512]{1,0:T(8,128)(2,1)}, bf16[1024,512]{1,0:T(8,128)(2,1)}, f32[2,1024]{1,0:T(2,128)}, f32[1024,1]{1,0:T(8,128)}, f32[1024,1]{1,0:T(8,128)}) custom-call(bf16[1024,512]{1,0:T(8,128)(2,1)} %get-tuple-element.358.refs_0_, bf16[1024,512]{1,0:T(8,128)(2,1)} %get-tuple-element.359.refs_1_, ...), custom_call_target="tpu_custom_call" | custom-call | flops 9126805504 | bytes 17825792 | tf_op jit(solution)/shard_map/dxn_partial/pallas_call | solution.py:329
  222.3 4.8 add_convert_fusion.1
  227.1 29.6 %dxn_partial.3 = (bf16[1024,512]{1,0:T(8,128)(2,1)}, bf16[1024,512]{1,0:T(8,128)(2,1)}, f32[2,1024]{1,0:T(2,128)}, f32[1024,1]{1,0:T(8,128)}, f32[1024,1]{1,0:T(8,128)}) custom-call(bf16[1024,512]{1,0:T(8,128)(2,1)} %get-tuple-element.358.refs_0_, bf16[1024,512]{1,0:T(8,128)(2,1)} %get-tuple-element.359.refs_1_, ...), custom_call_target="tpu_custom_call" | custom-call | flops 9126805504 | bytes 17825792 | tf_op jit(solution)/shard_map/dxn_partial/pallas_call | solution.py:329
  264.4 8.1 %weight_grad.10 = bf16[4,256,1408]{2,1,0:T(8,128)(2,1)} custom-call(s32[4]{0:T(128)} %get-tuple-element.481.order, bf16[1024,2048]{1,0:T(8,128)(2,1)} %lhs.5, bf16[512,1408]{1,0:T(8,128)(2,1)} %get-tuple-element.328.h_in.refs_0_, bf16[512,1408]{1,0:T(8,128)(2,1)} %get-tuple-element.329.h_in.refs_1_), custom_call_target="tpu_custom_call" | custom-call | flops 2952790016 | bytes 5767168 | tf_op jit(solution)/shard_map/weight_grad/pallas_call | solution.py:426
  275.9 21.2 %collective-permute-done.8 = bf16[1024,512]{1,0:T(8,128)(2,1)S(1)} collective-permute-done((bf16[1024,512]{1,0:T(8,128)(2,1)S(1)}, bf16[1024,512]{1,0:T(8,128)(2,1)S(1)}, u32[]{:S(2)}, u32[]{:S(2)}) %collective-permute-start.8) | collective-permute-done | bytes 1048608 | tf_op jit(solution)/shard_map/ppermute | solution.py:538
  298.6 5.6 weight_grad.11
  305.5 7.0 %collective-permute-start.7 = (bf16[1024,512]{1,0:T(8,128)(2,1)}, bf16[1024,512]{1,0:T(8,128)(2,1)}, u32[]{:S(2)}, u32[]{:S(2)}) collective-permute-start(bf16[1024,512]{1,0:T(8,128)(2,1)} %get-tuple-element.337), channel_id=1, source_target_pairs={{0,1},{3,2},{4,5},{7,6},{8,9},{11,10},{12,13},{15,14},{16,17},{19,... | collective-permute-start | bytes 3145736 | tf_op jit(solution)/shard_map/ppermute | solution.py:538
  312.5 9.0 %weight_grad.12 = (bf16[2,256,1408]{2,1,0:T(8,128)(2,1)}, bf16[2,256,1408]{2,1,0:T(8,128)(2,1)}) custom-call(s32[4]{0:T(128)} %get-tuple-element.480.order, s32[3,4]{1,0:T(4,128)} %constant.108.clone.slots, bf16[1024,2048]{1,0:T(8,128)(2,1)} %lhs.5, bf16[512,1408]{1,0:T(8,128)(2,1)} %get-tuple-element.328.h_in.refs_0_, ...), custom_call_target="tpu_custom_call" | custom-call | flops 2952790016 | bytes 5767168 | tf_op jit(solution)/shard_map/weight_grad/pallas_call | solution.py:426
  323.2 5.8 %weight_grad.13 = (bf16[2,256,512]{2,1,0:T(8,128)(2,1)}, bf16[2,256,512]{2,1,0:T(8,128)(2,1)}) custom-call(s32[4]{0:T(128)} %get-tuple-element.480.order, s32[3,4]{1,0:T(4,128)} %constant.108.clone.slots, bf16[1024,2048]{1,0:T(8,128)(2,1)} %lhs.5, bf16[512,512]{1,0:T(8,128)(2,1)} %get-tuple-element.333.o_in.refs_0_, ...), custom_call_target="tpu_custom_call" | custom-call | flops 1073741824 | bytes 2097152 | tf_op jit(solution)/shard_map/weight_grad/pallas_call | solution.py:426
  329.0 6.0 %collective-permute-done.7 = bf16[1024,512]{1,0:T(8,128)(2,1)} collective-permute-done((bf16[1024,512]{1,0:T(8,128)(2,1)}, bf16[1024,512]{1,0:T(8,128)(2,1)}, u32[]{:S(2)}, u32[]{:S(2)}) %collective-permute-start.7) | collective-permute-done | bytes 1048608 | tf_op jit(solution)/shard_map/ppermute | solution.py:538
  337.8 4.8 add_convert_fusion
  342.6 12.3 %collective-permute-done.5 = bf16[512,2048]{1,0:T(8,128)(2,1)} collective-permute-done((bf16[512,2048]{1,0:T(8,128)(2,1)}, bf16[512,2048]{1,0:T(8,128)(2,1)}, u32[]{:S(2)}, u32[]{:S(2)}) %collective-permute-start.5) | collective-permute-done | bytes 2097184 | tf_op jit(solution)/shard_map/ppermute | solution.py:557
  362.5 7.8 %weight_grad.14 = (bf16[4,256,512]{2,1,0:T(8,128)(2,1)}, bf16[4,256,512]{2,1,0:T(8,128)(2,1)}, bf16[4,256,512]{2,1,0:T(8,128)(2,1)}) custom-call(s32[4]{0:T(128)} %get-tuple-element.481.order, bf16[1024,2048]{1,0:T(8,128)(2,1)} %copy-done.6, bf16[1024,512]{1,0:T(8,128)(2,1)} %get-tuple-element.358.refs_0_, bf16[1024,512]{1,0:T(8,128)(2,1)} %get-tuple-element.359.refs_1_, ...), custom_call_target="tpu_custom_call" | custom-call | flops 3221225472 | bytes 6291456 | tf_op jit(solution)/shard_map/weight_grad/pallas_call | solution.py:426
  370.5 5.9 %collective-permute-start.23 = (bf16[1024,512]{1,0:T(8,128)(2,1)S(1)}, bf16[1024,512]{1,0:T(8,128)(2,1)}, u32[]{:S(2)}, u32[]{:S(2)}) collective-permute-start(bf16[1024,512]{1,0:T(8,128)(2,1)S(1)} %copy-done.17), channel_id=1, source_target_pairs={{0,1},{3,2},{4,5},{7,6},{8,9},{11,10},{12,13},{15,14},{16,17},{19,... | collective-permute-start | bytes 3145736 | tf_op jit(solution)/shard_map/ppermute | solution.py:538
  389.3 10.7 %weight_grad.15 = (bf16[2,256,512]{2,1,0:T(8,128)(2,1)}, bf16[2,256,512]{2,1,0:T(8,128)(2,1)}, bf16[2,256,512]{2,1,0:T(8,128)(2,1)}, bf16[2,256,512]{2,1,0:T(8,1...) custom-call(s32[4]{0:T(128)} %get-tuple-element.480.order, s32[9,4]{1,0:T(8,128)} %constant.109.clone.slots, ...), custom_call_target="tpu_custom_call" | custom-call | flops 3221225472 | bytes 6291456 | tf_op jit(solution)/shard_map/weight_grad/pallas_call | solution.py:426
  407.2 23.0 %collective-permute-done.20 = bf16[2,256,1408]{2,1,0:T(8,128)(2,1)} collective-permute-done((bf16[2,256,1408]{2,1,0:T(8,128)(2,1)}, bf16[2,256,1408]{2,1,0:T(8,128)(2,1)}, u32[]{:S(2)}, u32[]{:S(2)}) %collective-permute-start.20) | collective-permute-done | bytes 1441824 | tf_op jit(solution)/shard_map/ppermute | solution.py:496
  441.3 32.8 %collective-permute-done.17 = bf16[1024,512]{1,0:T(8,128)(2,1)S(1)} collective-permute-done((bf16[1024,512]{1,0:T(8,128)(2,1)S(1)}, bf16[1024,512]{1,0:T(8,128)(2,1)S(1)}, u32[]{:S(2)}, u32[]{:S(2)}) %collective-permute-start.17) | collective-permute-done | bytes 1048608 | tf_op jit(solution)/shard_map/ppermute | solution.py:557
  490.4 9.7 %collective-permute-done.32 = bf16[2,256,512]{2,1,0:T(8,128)(2,1)S(1)} collective-permute-done((bf16[2,256,512]{2,1,0:T(8,128)(2,1)S(1)}, bf16[2,256,512]{2,1,0:T(8,128)(2,1)S(1)}, u32[]{:S(2)}, u32[]{:S(2)}) %collective-permute-start.32) | collective-permute-done | bytes 524320 | tf_op jit(solution)/shard_map/ppermute | solution.py:496
  501.3 14.0 %collective-permute-done.29 = bf16[1,256,1408]{2,1,0:T(8,128)(2,1)S(1)} collective-permute-done((bf16[1,256,1408]{2,1,0:T(8,128)(2,1)S(1)}, bf16[1,256,1408]{2,1,0:T(8,128)(2,1)S(1)}, u32[]{:S(2)}, u32[]{:S(2)}) %collective-permute-start.29) | collective-permute-done | bytes 720928 | tf_op jit(solution)/shard_map/ppermute | solution.py:516
  554.3 12.1 %collective-permute-done.40 = bf16[1024,512]{1,0:T(8,128)(2,1)} collective-permute-done((bf16[1024,512]{1,0:T(8,128)(2,1)}, bf16[1024,512]{1,0:T(8,128)(2,1)}, u32[]{:S(2)}, u32[]{:S(2)}) %collective-permute-start.40) | collective-permute-done | bytes 1048608 | tf_op jit(solution)/shard_map/ppermute | solution.py:557
  (250 shorter events, 164.6 us)
Async XLA Ops:
  61.1 58.1 %collective-permute-start = (bf16[512,2048]{1,0:T(8,128)(2,1)}, bf16[512,2048]{1,0:T(8,128)(2,1)}, u32[]{:S(2)}, u32[]{:S(2)}) collective-permute-start(bf16[512,2048]{1,0:T(8,128)(2,1)} %out_partial.2), channel_id=1, source_target_pairs={{0,1},{3,2},{4,5},{7,6},{8,9},{11,10},{12,13},{15,14},{16,17},{19,... | collective-permute-start | bytes 6291464 | tf_op jit(solution)/shard_map/ppermute | solution.py:538
  135.4 82.1 %collective-permute-start.2 = (bf16[512,2048]{1,0:T(8,128)(2,1)S(1)}, bf16[512,2048]{1,0:T(8,128)(2,1)}, u32[]{:S(2)}, u32[]{:S(2)}) collective-permute-start(bf16[512,2048]{1,0:T(8,128)(2,1)S(1)} %copy-done.10), channel_id=1, source_target_pairs={{0,1},{3,2},{4,5},{7,6},{8,9},{11,10},{12,13},{15,14},{16,17},{19,... | collective-permute-start | bytes 6291464 | tf_op jit(solution)/shard_map/ppermute | solution.py:538
  140.1 80.6 %collective-permute-start.1 = (bf16[512,2048]{1,0:T(8,128)(2,1)}, bf16[512,2048]{1,0:T(8,128)(2,1)}, u32[]{:S(2)}, u32[]{:S(2)}) collective-permute-start(bf16[512,2048]{1,0:T(8,128)(2,1)} %add_convert_fusion.3), channel_id=1, source_target_pairs={{1,2},{2,1},{5,6},{6,5},{9,10},{10,9},{13,14},{14,13},{17,18},{18,... | collective-permute-start | bytes 6291464 | tf_op jit(solution)/shard_map/ppermute | solution.py:543
  163.4 97.6 %collective-permute-start.9 = (bf16[2,256,1408]{2,1,0:T(8,128)(2,1)}, bf16[2,256,1408]{2,1,0:T(8,128)(2,1)}, u32[]{:S(2)}, u32[]{:S(2)}) collective-permute-start(bf16[2,256,1408]{2,1,0:T(8,128)(2,1)} %get-tuple-element.268), channel_id=1, source_target_pairs={{0,8},{4,12},{8,0},{12,4},{16,24},{20,28},{24,16},{28,20},{1,9},{5... | collective-permute-start | bytes 4325384 | tf_op jit(solution)/shard_map/ppermute | solution.py:496
  220.7 40.4 %collective-permute-start.10 = (bf16[2,256,1408]{2,1,0:T(8,128)(2,1)}, bf16[2,256,1408]{2,1,0:T(8,128)(2,1)S(1)}, u32[]{:S(2)}, u32[]{:S(2)}) collective-permute-start(bf16[2,256,1408]{2,1,0:T(8,128)(2,1)} %get-tuple-element.296), channel_id=1, source_target_pairs={{0,16},{4,20},{8,24},{12,28},{16,0},{20,4},{24,8},{28,12},{1,17},{... | collective-permute-start | bytes 4325384 | tf_op jit(solution)/shard_map/ppermute | solution.py:496
  272.4 40.1 %collective-permute-start.12 = (bf16[4,256,1408]{2,1,0:T(8,128)(2,1)}, bf16[4,256,1408]{2,1,0:T(8,128)(2,1)}, u32[]{:S(2)}, u32[]{:S(2)}) collective-permute-start(bf16[4,256,1408]{2,1,0:T(8,128)(2,1)} %weight_grad.10), channel_id=1, source_target_pairs={{0,4},{4,0},{8,12},{12,8},{16,20},{20,16},{24,28},{28,24},{1,5},{5... | collective-permute-start | bytes 8650760 | tf_op jit(solution)/shard_map/ppermute | solution.py:479
  272.5 24.6 %collective-permute-start.8 = (bf16[1024,512]{1,0:T(8,128)(2,1)S(1)}, bf16[1024,512]{1,0:T(8,128)(2,1)S(1)}, u32[]{:S(2)}, u32[]{:S(2)}) collective-permute-start(bf16[1024,512]{1,0:T(8,128)(2,1)S(1)} %copy-done.18), channel_id=1, source_target_pairs={{0,1},{3,2},{4,5},{7,6},{8,9},{11,10},{12,13},{15,14},{16,17},{19,... | collective-permute-start | bytes 3145736 | tf_op jit(solution)/shard_map/ppermute | solution.py:538
  273.8 63.9 %collective-permute-start.6 = (bf16[512,2048]{1,0:T(8,128)(2,1)S(1)}, bf16[512,2048]{1,0:T(8,128)(2,1)}, u32[]{:S(2)}, u32[]{:S(2)}) collective-permute-start(bf16[512,2048]{1,0:T(8,128)(2,1)S(1)} %add_convert_fusion.2), channel_id=1, source_target_pairs={{1,2},{2,1},{5,6},{6,5},{9,10},{10,9},{13,14},{14,13},{17,18},{18,... | collective-permute-start | bytes 6291464 | tf_op jit(solution)/shard_map/ppermute | solution.py:543
  304.2 17.3 %collective-permute-start.11 = (bf16[4,256,512]{2,1,0:T(8,128)(2,1)}, bf16[4,256,512]{2,1,0:T(8,128)(2,1)}, u32[]{:S(2)}, u32[]{:S(2)}) collective-permute-start(bf16[4,256,512]{2,1,0:T(8,128)(2,1)} %weight_grad.11), channel_id=1, source_target_pairs={{0,4},{4,0},{8,12},{12,8},{16,20},{20,16},{24,28},{28,24},{1,5},{5... | collective-permute-start | bytes 3145736 | tf_op jit(solution)/shard_map/ppermute | solution.py:479
  304.2 50.6 %collective-permute-start.5 = (bf16[512,2048]{1,0:T(8,128)(2,1)}, bf16[512,2048]{1,0:T(8,128)(2,1)}, u32[]{:S(2)}, u32[]{:S(2)}) collective-permute-start(bf16[512,2048]{1,0:T(8,128)(2,1)} %add_convert_fusion.1), channel_id=1, source_target_pairs={{1,0},{2,3},{5,4},{6,7},{9,8},{10,11},{13,12},{14,15},{17,16},{18,... | collective-permute-start | bytes 6291464 | tf_op jit(solution)/shard_map/ppermute | solution.py:557
  305.5 29.4 %collective-permute-start.7 = (bf16[1024,512]{1,0:T(8,128)(2,1)}, bf16[1024,512]{1,0:T(8,128)(2,1)}, u32[]{:S(2)}, u32[]{:S(2)}) collective-permute-start(bf16[1024,512]{1,0:T(8,128)(2,1)} %get-tuple-element.337), channel_id=1, source_target_pairs={{0,1},{3,2},{4,5},{7,6},{8,9},{11,10},{12,13},{15,14},{16,17},{19,... | collective-permute-start | bytes 3145736 | tf_op jit(solution)/shard_map/ppermute | solution.py:538
  312.5 57.8 %collective-permute-start.15 = (f32[6144]{0:T(1024)S(1)}, f32[6144]{0:T(1024)S(1)}, u32[]{:S(2)}, u32[]{:S(2)}) collective-permute-start(f32[6144]{0:T(1024)S(1)} %copy-done.27), channel_id=1, source_target_pairs={{0,1},{1,0},{2,3},{3,2},{4,5},{5,4},{6,7},{7,6},{8,9},{9,8},{10,11... | collective-permute-start | bytes 73736 | tf_op jit(solution)/shard_map/ppermute | solution.py:571
  321.5 58.5 %collective-permute-start.14 = (bf16[1024,512]{1,0:T(8,128)(2,1)S(1)}, bf16[1024,512]{1,0:T(8,128)(2,1)}, u32[]{:S(2)}, u32[]{:S(2)}) collective-permute-start(bf16[1024,512]{1,0:T(8,128)(2,1)S(1)} %add_convert_fusion.11), channel_id=1, source_target_pairs={{1,2},{2,1},{5,6},{6,5},{9,10},{10,9},{13,14},{14,13},{17,18},{18,... | collective-permute-start | bytes 3145736 | tf_op jit(solution)/shard_map/ppermute | solution.py:543
  370.5 29.5 %collective-permute-start.23 = (bf16[1024,512]{1,0:T(8,128)(2,1)S(1)}, bf16[1024,512]{1,0:T(8,128)(2,1)}, u32[]{:S(2)}, u32[]{:S(2)}) collective-permute-start(bf16[1024,512]{1,0:T(8,128)(2,1)S(1)} %copy-done.17), channel_id=1, source_target_pairs={{0,1},{3,2},{4,5},{7,6},{8,9},{11,10},{12,13},{15,14},{16,17},{19,... | collective-permute-start | bytes 3145736 | tf_op jit(solution)/shard_map/ppermute | solution.py:538
  379.9 23.0 %collective-permute-start.21 = (bf16[1,256,1408]{2,1,0:T(8,128)(2,1)}, bf16[1,256,1408]{2,1,0:T(8,128)(2,1)}, u32[]{:S(2)}, u32[]{:S(2)}) collective-permute-start(bf16[1,256,1408]{2,1,0:T(8,128)(2,1)} %get-tuple-element.453), channel_id=1, source_target_pairs={{0,16},{4,20},{8,24},{12,28},{16,0},{20,4},{24,8},{28,12},{1,17},{... | collective-permute-start | bytes 2162696 | tf_op jit(solution)/shard_map/ppermute | solution.py:516
  380.5 21.9 %collective-permute-start.22 = (bf16[1,256,1408]{2,1,0:T(8,128)(2,1)}, bf16[1,256,1408]{2,1,0:T(8,128)(2,1)}, u32[]{:S(2)}, u32[]{:S(2)}) collective-permute-start(bf16[1,256,1408]{2,1,0:T(8,128)(2,1)} %get-tuple-element.450), channel_id=1, source_target_pairs={{0,8},{4,12},{8,0},{12,4},{16,24},{20,28},{24,16},{28,20},{1,9},{5... | collective-permute-start | bytes 2162696 | tf_op jit(solution)/shard_map/ppermute | solution.py:516
  385.5 93.9 %collective-permute-start.33 = (bf16[1024,512]{1,0:T(8,128)(2,1)}, bf16[1024,512]{1,0:T(8,128)(2,1)}, u32[]{:S(2)}, u32[]{:S(2)}) collective-permute-start(bf16[1024,512]{1,0:T(8,128)(2,1)} %get-tuple-element.389), channel_id=1, source_target_pairs={{0,1},{3,2},{4,5},{7,6},{8,9},{11,10},{12,13},{15,14},{16,17},{19,... | collective-permute-start | bytes 3145736 | tf_op jit(solution)/shard_map/ppermute | solution.py:538
  387.8 42.4 %collective-permute-start.20 = (bf16[2,256,1408]{2,1,0:T(8,128)(2,1)}, bf16[2,256,1408]{2,1,0:T(8,128)(2,1)}, u32[]{:S(2)}, u32[]{:S(2)}) collective-permute-start(bf16[2,256,1408]{2,1,0:T(8,128)(2,1)} %get-tuple-element.331), channel_id=1, source_target_pairs={{0,16},{4,20},{8,24},{12,28},{16,0},{20,4},{24,8},{28,12},{1,17},{... | collective-permute-start | bytes 4325384 | tf_op jit(solution)/shard_map/ppermute | solution.py:496
  400.0 33.3 %collective-permute-start.19 = (bf16[1024,512]{1,0:T(8,128)(2,1)}, bf16[1024,512]{1,0:T(8,128)(2,1)S(1)}, u32[]{:S(2)}, u32[]{:S(2)}) collective-permute-start(bf16[1024,512]{1,0:T(8,128)(2,1)} %add_convert_fusion.10), channel_id=1, source_target_pairs={{1,2},{2,1},{5,6},{6,5},{9,10},{10,9},{13,14},{14,13},{17,18},{18,... | collective-permute-start | bytes 3145736 | tf_op jit(solution)/shard_map/ppermute | solution.py:543
  402.4 38.0 %collective-permute-start.18 = (bf16[2,256,512]{2,1,0:T(8,128)(2,1)S(1)}, bf16[2,256,512]{2,1,0:T(8,128)(2,1)S(1)}, u32[]{:S(2)}, u32[]{:S(2)}) collective-permute-start(bf16[2,256,512]{2,1,0:T(8,128)(2,1)S(1)} %copy-done.35), channel_id=1, source_target_pairs={{0,16},{4,20},{8,24},{12,28},{16,0},{20,4},{24,8},{28,12},{1,17},{... | collective-permute-start | bytes 1572872 | tf_op jit(solution)/shard_map/ppermute | solution.py:496
  403.0 73.8 %collective-permute-start.13 = (bf16[512,2048]{1,0:T(8,128)(2,1)}, bf16[512,2048]{1,0:T(8,128)(2,1)S(1)}, u32[]{:S(2)}, u32[]{:S(2)}) collective-permute-start(bf16[512,2048]{1,0:T(8,128)(2,1)} %add_convert_fusion), channel_id=1, source_target_pairs={{1,0},{2,3},{5,4},{6,7},{9,8},{10,11},{13,12},{14,15},{17,16},{18,... | collective-permute-start | bytes 6291464 | tf_op jit(solution)/shard_map/ppermute | solution.py:557
  430.2 43.9 %collective-permute-start.17 = (bf16[1024,512]{1,0:T(8,128)(2,1)S(1)}, bf16[1024,512]{1,0:T(8,128)(2,1)S(1)}, u32[]{:S(2)}, u32[]{:S(2)}) collective-permute-start(bf16[1024,512]{1,0:T(8,128)(2,1)S(1)} %copy-done.8), channel_id=1, source_target_pairs={{1,0},{2,3},{5,4},{6,7},{9,8},{10,11},{13,12},{14,15},{17,16},{18,... | collective-permute-start | bytes 3145736 | tf_op jit(solution)/shard_map/ppermute | solution.py:557
  433.3 49.5 %collective-permute-start.30 = (bf16[2,256,512]{2,1,0:T(8,128)(2,1)S(1)}, bf16[2,256,512]{2,1,0:T(8,128)(2,1)S(1)}, u32[]{:S(2)}, u32[]{:S(2)}) collective-permute-start(bf16[2,256,512]{2,1,0:T(8,128)(2,1)S(1)} %copy-done.38), channel_id=1, source_target_pairs={{0,8},{4,12},{8,0},{12,4},{16,24},{20,28},{24,16},{28,20},{1,9},{5... | collective-permute-start | bytes 1572872 | tf_op jit(solution)/shard_map/ppermute | solution.py:496
  440.4 77.6 %collective-permute-start.28 = (bf16[1024,512]{1,0:T(8,128)(2,1)S(1)}, bf16[1024,512]{1,0:T(8,128)(2,1)S(1)}, u32[]{:S(2)}, u32[]{:S(2)}) collective-permute-start(bf16[1024,512]{1,0:T(8,128)(2,1)S(1)} %add_convert_fusion.8), channel_id=1, source_target_pairs={{1,2},{2,1},{5,6},{6,5},{9,10},{10,9},{13,14},{14,13},{17,18},{18,... | collective-permute-start | bytes 3145736 | tf_op jit(solution)/shard_map/ppermute | solution.py:543
  474.1 14.8 %collective-permute-start.31 = (bf16[2,256,512]{2,1,0:T(8,128)(2,1)S(1)}, bf16[2,256,512]{2,1,0:T(8,128)(2,1)S(1)}, u32[]{:S(2)}, u32[]{:S(2)}) collective-permute-start(bf16[2,256,512]{2,1,0:T(8,128)(2,1)S(1)} %copy-done.37), channel_id=1, source_target_pairs={{0,8},{4,12},{8,0},{12,4},{16,24},{20,28},{24,16},{28,20},{1,9},{5... | collective-permute-start | bytes 1572872 | tf_op jit(solution)/shard_map/ppermute | solution.py:496
  476.8 23.3 %collective-permute-start.32 = (bf16[2,256,512]{2,1,0:T(8,128)(2,1)S(1)}, bf16[2,256,512]{2,1,0:T(8,128)(2,1)S(1)}, u32[]{:S(2)}, u32[]{:S(2)}) collective-permute-start(bf16[2,256,512]{2,1,0:T(8,128)(2,1)S(1)} %copy-done.36), channel_id=1, source_target_pairs={{0,8},{4,12},{8,0},{12,4},{16,24},{20,28},{24,16},{28,20},{1,9},{5... | collective-permute-start | bytes 1572872 | tf_op jit(solution)/shard_map/ppermute | solution.py:496
  479.5 35.8 %collective-permute-start.29 = (bf16[1,256,1408]{2,1,0:T(8,128)(2,1)S(1)}, bf16[1,256,1408]{2,1,0:T(8,128)(2,1)S(1)}, u32[]{:S(2)}, u32[]{:S(2)}) collective-permute-start(bf16[1,256,1408]{2,1,0:T(8,128)(2,1)S(1)} %get-tuple-element.449), channel_id=1, source_target_pairs={{0,8},{4,12},{8,0},{12,4},{16,24},{20,28},{24,16},{28,20},{1,9},{5... | collective-permute-start | bytes 2162696 | tf_op jit(solution)/shard_map/ppermute | solution.py:516
  482.9 37.6 %collective-permute-start.27 = (bf16[1024,512]{1,0:T(8,128)(2,1)S(1)}, bf16[1024,512]{1,0:T(8,128)(2,1)S(1)}, u32[]{:S(2)}, u32[]{:S(2)}) collective-permute-start(bf16[1024,512]{1,0:T(8,128)(2,1)S(1)} %add_convert_fusion.7), channel_id=1, source_target_pairs={{1,0},{2,3},{5,4},{6,7},{9,8},{10,11},{13,12},{14,15},{17,16},{18,... | collective-permute-start | bytes 3145736 | tf_op jit(solution)/shard_map/ppermute | solution.py:557
  488.9 34.4 %collective-permute-start.39 = (bf16[1,256,512]{2,1,0:T(8,128)(2,1)S(1)}, bf16[1,256,512]{2,1,0:T(8,128)(2,1)S(1)}, u32[]{:S(2)}, u32[]{:S(2)}) collective-permute-start(bf16[1,256,512]{2,1,0:T(8,128)(2,1)S(1)} %get-tuple-element.455), channel_id=1, source_target_pairs={{0,8},{4,12},{8,0},{12,4},{16,24},{20,28},{24,16},{28,20},{1,9},{5... | collective-permute-start | bytes 786440 | tf_op jit(solution)/shard_map/ppermute | solution.py:516
  500.1 30.3 %collective-permute-start.35 = (bf16[1024,512]{1,0:T(8,128)(2,1)S(1)}, bf16[1024,512]{1,0:T(8,128)(2,1)S(1)}, u32[]{:S(2)}, u32[]{:S(2)}) collective-permute-start(bf16[1024,512]{1,0:T(8,128)(2,1)S(1)} %add_convert_fusion.6), channel_id=1, source_target_pairs={{1,2},{2,1},{5,6},{6,5},{9,10},{10,9},{13,14},{14,13},{17,18},{18,... | collective-permute-start | bytes 3145736 | tf_op jit(solution)/shard_map/ppermute | solution.py:543
  523.3 28.5 %collective-permute-start.34 = (bf16[1024,512]{1,0:T(8,128)(2,1)}, bf16[1024,512]{1,0:T(8,128)(2,1)}, u32[]{:S(2)}, u32[]{:S(2)}) collective-permute-start(bf16[1024,512]{1,0:T(8,128)(2,1)} %add_convert_fusion.5), channel_id=1, source_target_pairs={{1,0},{2,3},{5,4},{6,7},{9,8},{10,11},{13,12},{14,15},{17,16},{18,... | collective-permute-start | bytes 3145736 | tf_op jit(solution)/shard_map/ppermute | solution.py:557
  532.3 34.0 %collective-permute-start.40 = (bf16[1024,512]{1,0:T(8,128)(2,1)}, bf16[1024,512]{1,0:T(8,128)(2,1)}, u32[]{:S(2)}, u32[]{:S(2)}) collective-permute-start(bf16[1024,512]{1,0:T(8,128)(2,1)} %add_convert_fusion.4), channel_id=1, source_target_pairs={{1,0},{2,3},{5,4},{6,7},{9,8},{10,11},{13,12},{14,15},{17,16},{18,... | collective-permute-start | bytes 3145736 | tf_op jit(solution)/shard_map/ppermute | solution.py:557
  (57 other events, 582.4 us)
